TPU v7x, 32 devices: a whole 2x2x4 slice. The times are simulated.
32 devices in a mesh: groups: 2 (over x), scene: 16 (over z, y, core).
Axes of the slice: x: 2, y: 2, z: 4, core: 2. Of those that a mesh axis runs over, the one named last changes fastest.
Arguments:
- tokens: bfloat16 [32, 196, 768], P(('groups', 'scene')), parts along dimension 0, may hold values from -6 to 6
- qkv_weight: bfloat16 [768, 2304], replicated, may hold values from -0.21875 to 0.21875
- out_weight: bfloat16 [768, 768], replicated, may hold values from -0.21875 to 0.21875
- attn_gain: float32 [768], replicated, may hold values from 0.1 to 1.9
- head_gain: float32 [768], replicated, may hold values from 0.1 to 1.9
- head_weight: bfloat16 [768, 1024], replicated, may hold values from -0.21875 to 0.21875
- head_bias: float32 [1024], replicated, may hold values from -3 to 3
- pair_list: int32 [64, 2], P('groups'), parts along dimension 0, may hold values from 0 to 15, as said below
- pair_count: int32 [32], P('groups'), parts along dimension 0, may hold values from 1 to 2, as said below
Outputs:
- joined: float32 [32, 196, 768], P(('groups', 'scene')), parts along dimension 0
There are 2 independent parts, one for each index of `groups`. A program takes and returns all parts, laid end to end along the dimension named above; an argument that names none is the same for every part. Nothing has to cross between parts.
Inputs may be any that keep to these rules, and one draw needn't show every extreme that they name: `pair_list`: slot j of device d (row d * 2 + j) holds a pair whose first image is d + (j mod 1); its second image is owned by a device 1 to 2 places away along the scene axis taken as a cycle, image i being owned by device i. `pair_count`: entry d is the number of live slots of device d; slots from that number on are ignored. In every draw some device has exactly 2 and another exactly 1.
All inputs are finite; a program needn't handle non-finite values.
Results may differ from a plain program's by a relative error of at most 0.0045.
Values may be sent and summed in bfloat16 or wider, within the bound.
No kernel may reach another device: no remote copies, remote signals or barrier semaphores. Data moves between devices by JAX's collectives and lax.ppermute only.
A program may use at most 128 MiB of HBM per device.

v0:
```python
import jax
import jax.numpy as jnp
from jax import lax
from jax.sharding import PartitionSpec as P

HEADS = 12
REACH = 2


TEMPER = 16.0
CONF_RANGE = 4.0
EPSILON = 1e-06


def shifted(value, axis, steps):
    count = lax.axis_size(axis)
    pairs = [(source, (source + steps) % count) for source in range(count)]
    return lax.ppermute(value, axis, pairs)


def layer_norm(values, gain_vec):
    centred = values - jnp.mean(values, axis=-1, keepdims=True)
    spread = jnp.mean(centred * centred, axis=-1, keepdims=True)
    return centred * lax.rsqrt(spread + EPSILON) * gain_vec


def head_unit(values):
    shaped = values.reshape(values.shape[:-1] + (HEADS, values.shape[-1] // HEADS))
    energy = jnp.mean(shaped * shaped, axis=-1, keepdims=True)
    return (shaped * lax.rsqrt(energy + EPSILON)).reshape(values.shape)


def normed_rows(token_rows, attn_gain):
    return layer_norm(token_rows.astype(jnp.float32), attn_gain).astype(jnp.bfloat16)


def queries_of(normed, weight_cols):
    mixed = jnp.einsum("vtd,de->vte", normed, weight_cols, preferred_element_type=jnp.float32)
    return head_unit(mixed).astype(jnp.bfloat16)


def keys_values_of(normed, weight_cols):
    model_width = normed.shape[-1]
    mixed = jnp.einsum("vtd,de->vte", normed, weight_cols, preferred_element_type=jnp.float32)
    return (
        head_unit(mixed[..., :model_width]).astype(jnp.bfloat16),
        mixed[..., model_width:].astype(jnp.bfloat16),
    )


def view_maps(own_rows, queries, key_rows, values, out_weight, head_gain, head_weight, head_bias):
    view_count, token_count, model_width = own_rows.shape
    head_size = model_width // HEADS
    query_heads = queries.reshape(view_count, token_count, HEADS, head_size)
    key_heads = key_rows.reshape(view_count, token_count, HEADS, head_size)
    value_heads = values.reshape(view_count, token_count, HEADS, head_size)
    scores = jnp.einsum(
        "vthc,vshc->vhts", query_heads, key_heads, preferred_element_type=jnp.float32
    ) * (TEMPER / head_size)
    exponent = jnp.exp(scores)
    attention = (exponent / jnp.sum(exponent, axis=-1, keepdims=True)).astype(jnp.bfloat16)
    attended = jnp.einsum(
        "vhts,vshc->vthc", attention, value_heads, preferred_element_type=jnp.float32
    )
    attended = attended.reshape(view_count, token_count, model_width).astype(jnp.bfloat16)
    mixed = own_rows.astype(jnp.float32) + jnp.einsum(
        "vtd,de->vte", attended, out_weight, preferred_element_type=jnp.float32
    )
    head_in = layer_norm(mixed, head_gain).astype(jnp.bfloat16)
    head_out = (
        jnp.einsum("vtd,de->vte", head_in, head_weight, preferred_element_type=jnp.float32)
        + head_bias
    )
    xyz_cols = 3 * (head_weight.shape[1] // 4)
    return (
        head_out[..., :xyz_cols].astype(jnp.bfloat16),
        head_out[..., xyz_cols:].astype(jnp.bfloat16),
    )


def contributions(xyz, conf, image_ids, live_mask, first_id, span_count):
    view_count, token_count, xyz_cols = xyz.shape
    pixels = conf.shape[-1]
    local_ids = image_ids - first_id
    onehot = (local_ids[None, :] == jnp.arange(span_count, dtype=jnp.int32)[:, None]).astype(
        jnp.float32
    ) * live_mask[None, :]
    weight = jnp.exp(CONF_RANGE * jnp.tanh(conf.astype(jnp.float32) / CONF_RANGE))
    weighted = (
        weight[:, :, None, :] * xyz.astype(jnp.float32).reshape(view_count, token_count, 3, pixels)
    ).reshape(view_count, token_count, xyz_cols)
    weighted_sum = jnp.einsum("iv,vtx->itx", onehot, weighted, precision=lax.Precision.HIGHEST)
    weight_sum = jnp.einsum("iv,vtp->itp", onehot, weight, precision=lax.Precision.HIGHEST)
    return (weighted_sum, weight_sum)


def per_device(
    tokens,
    qkv_weight,
    out_weight,
    attn_gain,
    head_gain,
    head_weight,
    head_bias,
    pair_list,
    pair_count,
):
    image_count, token_count, model_width = tokens.shape
    scene_size = lax.axis_size("scene")
    position = lax.axis_index("scene")
    pair_slots = pair_list.shape[0] // scene_size
    my_pairs = lax.dynamic_slice_in_dim(pair_list, position * pair_slots, pair_slots, 0)
    own_ids = jnp.concatenate([my_pairs[:, 0], my_pairs[:, 1]])
    partner_ids = jnp.concatenate([my_pairs[:, 1], my_pairs[:, 0]])
    cycle_images = scene_size * image_count
    window_start = (position - REACH) * image_count
    own_local = (own_ids - window_start) % cycle_images
    partner_local = (partner_ids - window_start) % cycle_images
    blocks = []
    for offset in range(-REACH, REACH + 1):
        if offset == 0:
            blocks.append(tokens)
        else:
            blocks.append(shifted(tokens, "scene", -offset))
    window = jnp.concatenate(blocks, axis=0)
    own_rows = window[own_local]
    partner_rows = window[partner_local]
    queries = queries_of(normed_rows(own_rows, attn_gain), qkv_weight[:, :model_width])
    key_rows, values = keys_values_of(
        normed_rows(partner_rows, attn_gain), qkv_weight[:, model_width:]
    )
    xyz, conf = view_maps(
        own_rows, queries, key_rows, values, out_weight, head_gain, head_weight, head_bias
    )
    slot_live = (jnp.arange(pair_slots, dtype=jnp.int32) < pair_count[position]).astype(jnp.float32)
    live_mask = jnp.concatenate([slot_live, slot_live])
    window_sum, window_weight = contributions(
        xyz, conf, own_local, live_mask, 0, (2 * REACH + 1) * image_count
    )
    middle = REACH * image_count
    weighted_sum = window_sum[middle : middle + image_count]
    weight_sum = window_weight[middle : middle + image_count]
    for offset in range(-REACH, REACH + 1):
        if offset != 0:
            row_start = (offset + REACH) * image_count
            arrived_sum, arrived_weight = (
                shifted(
                    window_sum[row_start : row_start + image_count].astype(jnp.bfloat16),
                    "scene",
                    offset,
                ).astype(jnp.float32),
                shifted(
                    window_weight[row_start : row_start + image_count].astype(jnp.bfloat16),
                    "scene",
                    offset,
                ).astype(jnp.float32),
            )
            weighted_sum = weighted_sum + arrived_sum
            weight_sum = weight_sum + arrived_weight
    return weighted_sum / jnp.tile(weight_sum, (1, 1, 3))


def solution(mesh):
    return jax.shard_map(
        per_device,
        mesh=mesh,
        in_specs=(
            P(("groups", "scene"), None, None),
            P(),
            P(),
            P(),
            P(),
            P(),
            P(),
            P("groups", None),
            P("groups"),
        ),
        out_specs=P(("groups", "scene"), None, None),
        check_vma=False,
    )
```

profile of v0, /device:TPU:0, one launch (start us, length us, event | category | flops | bytes accessed | tf_op | source)
XLA Modules:
  0.0 148.5 jit_solution(17032723547600941379)
XLA Ops:
  0.0 5.5 %collective-permute-start.2 = (bf16[1,196,768]{2,1,0:T(8,128)(2,1)}, bf16[1,196,768]{2,1,0:T(8,128)(2,1)S(1)}, u32[]{:S(2)}, u32[]{:S(2)}) collective-permute-start(bf16[1,196,768]{2,1,0:T(8,128)(2,1)} %param.9), channel_id=1, source_target_pairs={{0,15},{1,0},{2,1},{3,2},{4,3},{5,4},{6,5},{7,6},{8,7},{9,8},{10,9... | collective-permute-start | bytes 903176 | tf_op jit(solution)/shard_map/ppermute | solution.py:18
  5.5 4.7 %collective-permute-start.3 = (bf16[1,196,768]{2,1,0:T(8,128)(2,1)}, bf16[1,196,768]{2,1,0:T(8,128)(2,1)S(1)}, u32[]{:S(2)}, u32[]{:S(2)}) collective-permute-start(bf16[1,196,768]{2,1,0:T(8,128)(2,1)} %param.9), channel_id=1, source_target_pairs={{0,14},{1,15},{2,0},{3,1},{4,2},{5,3},{6,4},{7,5},{8,6},{9,7},{10,... | collective-permute-start | bytes 903176 | tf_op jit(solution)/shard_map/ppermute | solution.py:18
  10.2 1.2 dynamic_slice.7
  13.1 8.2 %collective-permute-done = bf16[1,196,768]{2,1,0:T(8,128)(2,1)S(1)} collective-permute-done((bf16[1,196,768]{2,1,0:T(8,128)(2,1)}, bf16[1,196,768]{2,1,0:T(8,128)(2,1)S(1)}, u32[]{:S(2)}, u32[]{:S(2)}) %collective-permute-start) | collective-permute-done | bytes 301088 | tf_op jit(solution)/shard_map/ppermute | solution.py:18
  21.4 1.0 constant_dynamic-update-slice_fusion.2
  22.4 2.1 %collective-permute-done.3 = bf16[1,196,768]{2,1,0:T(8,128)(2,1)S(1)} collective-permute-done((bf16[1,196,768]{2,1,0:T(8,128)(2,1)}, bf16[1,196,768]{2,1,0:T(8,128)(2,1)S(1)}, u32[]{:S(2)}, u32[]{:S(2)}) %collective-permute-start.3) | collective-permute-done | bytes 301088 | tf_op jit(solution)/shard_map/ppermute | solution.py:18
  24.5 1.2 copy-done.2
  25.7 2.0 %gather_fusion.1 = bf16[4,196,768]{2,1,0:T(8,128)(2,1)S(1)} fusion(bf16[5,196,768]{2,1,0:T(8,128)(2,1)} %copy-done.2, s32[1024]{0:T(1024)S(1)} %get-tuple-element.29), kind=kCustom, calls=%fused_computation.1 | custom fusion | bytes 2408464 | tf_op jit(solution)/shard_map/gather | solution.py:127
  28.5 4.0 %fusion.14 = f32[4,196,1536]{2,1,0:T(8,128)S(1)} fusion(bf16[768,2304]{1,0:T(8,128)(2,1)} %param.10, bf16[4,196,768]{2,1,0:T(8,128)(2,1)S(1)} %gather_fusion.1, f32[768]{0:T(1024)S(1)} %copy-done.5, f32[4,196]{1,0:T(4,128)S(1)} %add_rsqrt_fusion.4, f32[4,196]{1,0:T(4,128)S(1)} %broadcast_multiply_fusion.2), kind=kOutput, calls=%fused_computation.30 | convolution fusion | flops 1852698624 | bytes 8389760 | tf_op jit(solution)/shard_map/vtd,de->vte/dot_general | solution.py:44
  32.5 1.3 slice.132
  33.8 2.1 %slice_multiply_fusion = f32[4,196,768]{2,1,0:T(8,128)} fusion(f32[4,196,1536]{2,1,0:T(8,128)S(1)} %fusion.14), kind=kLoop, calls=%fused_computation.33 | loop fusion | flops 602112 | bytes 4816896 | tf_op jit(solution)/shard_map/mul | solution.py:29
  35.9 2.0 %gather_fusion = bf16[4,196,768]{2,1,0:T(8,128)(2,1)S(1)} fusion(bf16[5,196,768]{2,1,0:T(8,128)(2,1)} %copy-done.2, s32[1024]{0:T(1024)S(1)} %get-tuple-element.30), kind=kCustom, calls=%fused_computation | custom fusion | bytes 2408464 | tf_op jit(solution)/shard_map/gather | solution.py:126
  38.7 2.5 %copy.29 = bf16[4,196,768]{1,2,0:T(8,128)(2,1)} copy(bf16[4,196,768]{2,1,0:T(8,128)(2,1)} %slice.132) | data formatting | bytes 2408448 | tf_op jit(solution)/shard_map/slice | solution.py:47
  41.2 3.4 %copy.33 = f32[4,196,768]{1,2,0:T(8,128)} copy(f32[4,196,768]{2,1,0:T(8,128)} %slice_multiply_fusion) | data formatting | bytes 4816896 | tf_op jit(solution)/shard_map/mul | solution.py:29
  44.6 2.3 %reduce_sum.86 = f32[4,196,12]{1,2,0:T(8,128)S(1)} reduce(f32[4,196,12,64]{1,3,2,0:T(8,128)} %bitcast.54, f32[]{:T(128)} %constant.52.clone.1), dimensions={3}, to_apply=%region_5.6 | reduce | flops 592704 | bytes 2446084 | tf_op jit(solution)/shard_map/reduce_sum | solution.py:29
  46.9 1.9 %mul.139 = f32[4,196,12,64]{1,3,2,0:T(8,128)} broadcast(f32[4,196,12]{1,2,0:T(8,128)S(1)} %add_rsqrt_fusion), dimensions={0,1,2} | broadcast | bytes 2446080 | tf_op jit(solution)/shard_map/mul | solution.py:30
  48.8 3.4 %copy.34 = f32[4,196,768]{2,1,0:T(8,128)} copy(f32[4,196,768]{1,2,0:T(8,128)} %bitcast.51) | data formatting | bytes 4816896 | tf_op jit(solution)/shard_map/mul | solution.py:30
  52.2 3.7 %multiply_convert_fusion.1 = bf16[4,196,768]{2,1,0:T(8,128)(2,1)} fusion(f32[4,196,768]{2,1,0:T(8,128)} %copy.34, f32[4,196,1536]{2,1,0:T(8,128)} %copy-done.1), kind=kLoop, calls=%fused_computation.26 | loop fusion | flops 1204224 | bytes 6021120 | tf_op jit(solution)/shard_map/convert_element_type | solution.py:46
  55.9 2.6 %copy.35 = bf16[4,196,768]{1,2,0:T(8,128)(2,1)} copy(bf16[4,196,768]{2,1,0:T(8,128)(2,1)} %multiply_convert_fusion.1) | data formatting | bytes 2408448 | tf_op jit(solution)/shard_map/convert_element_type | solution.py:46
  58.5 4.8 %fusion.62 = (f32[4,196,768]{2,1,0:T(8,128)}, f32[4,196,768]{2,1,0:T(8,128)}) fusion(bf16[768,2304]{1,0:T(8,128)(2,1)} %param.10, bf16[4,196,768]{2,1,0:T(8,128)(2,1)S(1)} %gather_fusion, f32[4,196]{1,0:T(4,128)S(1)} %add_rsqrt_fusion.3, f32[4,196]{1,0:T(4,128)S(1)} %broadcast_multiply_fusion.1, f32[768]{0:T(1024)S(1)} %copy-done.5), kind=kOutput, calls=%fused_computation.121 | convolution fusion | flops 928456704 | bytes 7210112 | tf_op jit(solution)/shard_map/vtd,de->vte/dot_general | solution.py:38
  63.3 3.4 %copy.30 = f32[4,196,768]{1,2,0:T(8,128)} copy(f32[4,196,768]{2,1,0:T(8,128)} %get-tuple-element.19) | data formatting | bytes 4816896 | tf_op jit(solution)/shard_map/mul | solution.py:29
  66.7 2.3 %reduce_sum.85 = f32[4,196,12]{1,2,0:T(8,128)S(1)} reduce(f32[4,196,12,64]{1,3,2,0:T(8,128)} %bitcast.53, f32[]{:T(128)} %constant.52.clone.1), dimensions={3}, to_apply=%region_4.5 | reduce | flops 592704 | bytes 2446084 | tf_op jit(solution)/shard_map/reduce_sum | solution.py:29
  69.0 1.9 %mul.134 = f32[4,196,12,64]{1,3,2,0:T(8,128)} broadcast(f32[4,196,12]{1,2,0:T(8,128)S(1)} %add_rsqrt_fusion.1), dimensions={0,1,2} | broadcast | bytes 2446080 | tf_op jit(solution)/shard_map/mul | solution.py:30
  70.9 3.4 %copy.31 = f32[4,196,768]{2,1,0:T(8,128)} copy(f32[4,196,768]{1,2,0:T(8,128)} %bitcast.52) | data formatting | bytes 4816896 | tf_op jit(solution)/shard_map/mul | solution.py:30
  74.2 3.7 %multiply_convert_fusion.2 = bf16[4,196,768]{2,1,0:T(8,128)(2,1)} fusion(f32[4,196,768]{2,1,0:T(8,128)} %get-tuple-element.20, f32[4,196,768]{2,1,0:T(8,128)} %copy.31), kind=kLoop, calls=%fused_computation.27 | loop fusion | flops 1204224 | bytes 6021120 | tf_op jit(solution)/shard_map/convert_element_type | solution.py:39
  77.9 2.5 %copy.32 = bf16[4,196,768]{1,2,0:T(8,128)(2,1)} copy(bf16[4,196,768]{2,1,0:T(8,128)(2,1)} %multiply_convert_fusion.2) | data formatting | bytes 2408448 | tf_op jit(solution)/shard_map/convert_element_type | solution.py:39
  80.5 4.2 %fusion = (f32[4,12,196]{2,1,0:T(8,128)S(1)}, f32[4,12,196,196]{2,3,1,0:T(8,128)S(1)}) fusion(bf16[4,196,12,64]{1,3,2,0:T(8,128)(2,1)} %bitcast.56, bf16[4,196,12,64]{1,3,2,0:T(8,128)(2,1)} %bitcast.55), kind=kOutput, calls=%fused_computation.4 | convolution fusion | flops 239706432 | bytes 9821952 | tf_op jit(solution)/shard_map/vthc,vshc->vhts/dot_general | solution.py:57
  84.7 2.3 %fusion.17 = bf16[4,12,64,196]{3,2,1,0:T(8,128)(2,1)S(1)} fusion(bf16[4,196,12,64]{1,3,2,0:T(8,128)(2,1)S(1)} %bitcast.57, f32[4,12,196,196]{2,3,1,0:T(8,128)S(1)} %get-tuple-element.22, f32[4,12,196]{2,1,0:T(8,128)S(1)} %get-tuple-element.21), kind=kOutput, calls=%fused_computation.34 | convolution fusion | flops 242161920 | bytes 9821952 | tf_op jit(solution)/shard_map/vhts,vshc->vthc/dot_general | solution.py:62
  87.0 1.4 fusion.63
  89.1 1.6 %add_convert_fusion = bf16[4,196,1024]{2,1,0:T(8,128)(2,1)S(1)} fusion(f32[1024]{0:T(1024)S(1)} %copy-done.7, bf16[768,1024]{1,0:T(8,128)(2,1)S(1)} %copy-done, f32[4,196,768]{2,1,0:T(8,128)S(1)} %get-tuple-element.24, f32[768]{0:T(1024)S(1)} %copy-done.8, f32[4,196]{1,0:T(4,128)S(1)} %add_rsqrt_fusion.2, f32[4,196]{1,0:T(4,128)S(1)} %broadcast_multiply_fusion), kind=kOutput, calls=%fused_computation.9 | convolution fusion | flops 1237139456 | bytes 5600384 | tf_op jit(solution)/shard_map/vtd,de->vte/dot_general | solution.py:71
  91.0 2.0 %fusion.65 = (bf16[5,196,256]{2,0,1:T(8,128)(2,1)S(1)}, f32[5,196,256]{2,0,1:T(8,128)S(1)}) fusion(f32[4,196,256]{2,1,0:T(8,128)S(1)} %multiply_exponential_fusion.1, f32[4]{0:T(128)S(1)} %add_convert_fusion.1, s32[4]{0:T(128)S(1)} %and_select_fusion.2), kind=kOutput, calls=%fused_computation.124 | convolution fusion | flops 12293160 | bytes 2308128 | tf_op jit(solution)/shard_map/iv,vtp->itp/dot_general | solution.py:93
  92.9 1.5 fusion.61
  94.4 3.4 %collective-permute-start.8 = (bf16[1,196,256]{2,0,1:T(2,128)(2,1)}, bf16[1,196,256]{2,0,1:T(2,128)(2,1)}, u32[]{:S(2)}, u32[]{:S(2)}) collective-permute-start(bf16[1,196,256]{2,0,1:T(2,128)(2,1)} %get-tuple-element.9), channel_id=1, source_target_pairs={{0,14},{1,15},{2,0},{3,1},{4,2},{5,3},{6,4},{7,5},{8,6},{9,7},{10,... | collective-permute-start | bytes 301064 | tf_op jit(solution)/shard_map/ppermute | solution.py:18
  97.8 1.8 %collective-permute-start.10 = (bf16[1,196,256]{2,0,1:T(2,128)(2,1)}, bf16[1,196,256]{2,0,1:T(2,128)(2,1)}, u32[]{:S(2)}, u32[]{:S(2)}) collective-permute-start(bf16[1,196,256]{2,0,1:T(2,128)(2,1)} %get-tuple-element.11), channel_id=1, source_target_pairs={{0,1},{1,2},{2,3},{3,4},{4,5},{5,6},{6,7},{7,8},{8,9},{9,10},{10,1... | collective-permute-start | bytes 301064 | tf_op jit(solution)/shard_map/ppermute | solution.py:18
  99.6 4.0 %collective-permute-start.9 = (bf16[1,196,256]{2,0,1:T(2,128)(2,1)}, bf16[1,196,256]{2,0,1:T(2,128)(2,1)}, u32[]{:S(2)}, u32[]{:S(2)}) collective-permute-start(bf16[1,196,256]{2,0,1:T(2,128)(2,1)} %get-tuple-element.12), channel_id=1, source_target_pairs={{0,15},{1,0},{2,1},{3,2},{4,3},{5,4},{6,5},{7,6},{8,7},{9,8},{10,9... | collective-permute-start | bytes 301064 | tf_op jit(solution)/shard_map/ppermute | solution.py:18
  103.7 2.2 %mul.150 = f32[4,196,3,256]{3,2,1,0:T(4,128)} broadcast(f32[4,196,256]{2,1,0:T(8,128)S(1)} %multiply_exponential_fusion.1), dimensions={0,1,3} | broadcast | bytes 3211264 | tf_op jit(solution)/shard_map/mul | solution.py:90
  105.9 4.8 %mul.151 = f32[4,196,768]{2,1,0:T(8,128)} reshape(f32[4,196,3,256]{3,2,1,0:T(4,128)} %mul.150) | data formatting | bytes 4816896 | tf_op jit(solution)/shard_map/mul | solution.py:90
  110.7 2.3 %convert_multiply_fusion = f32[4,196,768]{2,1,0:T(8,128)S(1)} fusion(f32[4,196,768]{2,1,0:T(8,128)} %mul.151, bf16[4,196,1024]{2,1,0:T(8,128)(2,1)} %copy-done.3), kind=kLoop, calls=%fused_computation.23 | loop fusion | flops 1204224 | bytes 6021120 | tf_op jit(solution)/shard_map/mul | solution.py:90
  113.0 7.0 %fusion.64 = (bf16[5,196,768]{2,0,1:T(8,128)(2,1)S(1)}, f32[5,196,768]{2,0,1:T(8,128)}) fusion(f32[4,196,768]{2,1,0:T(8,128)S(1)} %convert_multiply_fusion, f32[4]{0:T(128)S(1)} %add_convert_fusion.1, s32[4]{0:T(128)S(1)} %and_select_fusion.2), kind=kOutput, calls=%fused_computation.123 | convolution fusion | flops 36879400 | bytes 6924320 | tf_op jit(solution)/shard_map/iv,vtx->itx/dot_general | solution.py:92
  120.0 1.8 %fusion.60 = (bf16[1,196,768]{2,0,1:T(2,128)(2,1)S(1)}, bf16[1,196,768]{2,0,1:T(2,128)(2,1)S(1)}, bf16[1,196,768]{2,0,1:T(2,128)(2,1)S(1)}, bf16[1,196,768]{2,0,1:T(2,128)(2,1)S(1)}) fusion(bf16[5,196,768]{2,0,1:T(8,128)(2,1)S(1)} %get-tuple-element.25), kind=kLoop, calls=%fused_computation.119 | loop fusion | bytes 2408448 | tf_op jit(solution)/shard_map/slice | solution.py:148
  122.6 0.8 copy.43
  124.7 4.7 %collective-permute-start.4 = (bf16[1,196,768]{2,1,0:T(8,128)(2,1)S(1)}, bf16[1,196,768]{2,1,0:T(8,128)(2,1)}, u32[]{:S(2)}, u32[]{:S(2)}) collective-permute-start(bf16[1,196,768]{2,1,0:T(8,128)(2,1)S(1)} %copy.39), channel_id=1, source_target_pairs={{0,14},{1,15},{2,0},{3,1},{4,2},{5,3},{6,4},{7,5},{8,6},{9,7},{10,... | collective-permute-start | bytes 903176 | tf_op jit(solution)/shard_map/ppermute | solution.py:18
  129.4 1.9 %convert_add_fusion.1 = f32[1,196,256]{2,0,1:T(1,128)S(1)} fusion(bf16[1,196,256]{2,0,1:T(2,128)(2,1)} %collective-permute-done.11, bf16[1,196,256]{2,0,1:T(2,128)(2,1)} %collective-permute-done.10, bf16[1,196,256]{2,0,1:T(2,128)(2,1)} %collective-permute-done.9, bf16[1,196,256]{2,0,1:T(2,128)(2,1)} %collective-permute-done.8, ...), kind=kLoop, calls=%fused_computation.65 | loop fusion | flops 401408 | bytes 802816 | tf_op jit(solution)/shard_map/add | solution.py:159
  131.4 0.8 tile.14
  132.3 4.4 %collective-permute-done.6 = bf16[1,196,768]{2,1,0:T(8,128)(2,1)} collective-permute-done((bf16[1,196,768]{2,1,0:T(8,128)(2,1)}, bf16[1,196,768]{2,1,0:T(8,128)(2,1)}, u32[]{:S(2)}, u32[]{:S(2)}) %collective-permute-start.6) | collective-permute-done | bytes 301088 | tf_op jit(solution)/shard_map/ppermute | solution.py:18
  136.7 1.9 %collective-permute-done.7 = bf16[1,196,768]{2,1,0:T(8,128)(2,1)} collective-permute-done((bf16[1,196,768]{2,1,0:T(8,128)(2,1)}, bf16[1,196,768]{2,1,0:T(8,128)(2,1)}, u32[]{:S(2)}, u32[]{:S(2)}) %collective-permute-start.7) | collective-permute-done | bytes 301088 | tf_op jit(solution)/shard_map/ppermute | solution.py:18
  138.6 5.5 %collective-permute-done.4 = bf16[1,196,768]{2,1,0:T(8,128)(2,1)} collective-permute-done((bf16[1,196,768]{2,1,0:T(8,128)(2,1)S(1)}, bf16[1,196,768]{2,1,0:T(8,128)(2,1)}, u32[]{:S(2)}, u32[]{:S(2)}) %collective-permute-start.4) | collective-permute-done | bytes 301088 | tf_op jit(solution)/shard_map/ppermute | solution.py:18
  144.1 4.4 %fusion.39 = f32[1,196,768]{2,0,1:T(1,128)} fusion(f32[1,196,768]{2,0,1:T(1,128)S(1)} %tile.14, bf16[1,196,768]{2,1,0:T(8,128)(2,1)} %collective-permute-done.7, bf16[1,196,768]{2,1,0:T(8,128)(2,1)} %collective-permute-done.6, bf16[1,196,768]{2,1,0:T(8,128)(2,1)} %collective-permute-done.5, bf16[1,196,768]{2,1,0:T(8,128)(2,1)} %collective-permute-done.4, ...), kind=kLoop, calls=%fused_computation.57 | loop fusion | flops 1354752 | bytes 3010560 | tf_op jit(solution)/shard_map/div | solution.py:160
  (60 shorter events, 6.5 us)
Async XLA Ops:
  0.0 88.9 %copy-start = (bf16[768,1024]{1,0:T(8,128)(2,1)S(1)}, bf16[768,1024]{1,0:T(8,128)(2,1)}, u32[]{:S(2)}) copy-start(bf16[768,1024]{1,0:T(8,128)(2,1)} %param.14) | copy-start | bytes 4718596
  0.0 22.3 %collective-permute-start.2 = (bf16[1,196,768]{2,1,0:T(8,128)(2,1)}, bf16[1,196,768]{2,1,0:T(8,128)(2,1)S(1)}, u32[]{:S(2)}, u32[]{:S(2)}) collective-permute-start(bf16[1,196,768]{2,1,0:T(8,128)(2,1)} %param.9), channel_id=1, source_target_pairs={{0,15},{1,0},{2,1},{3,2},{4,3},{5,4},{6,5},{7,6},{8,7},{9,8},{10,9... | collective-permute-start | bytes 903176 | tf_op jit(solution)/shard_map/ppermute | solution.py:18
  5.5 15.8 %collective-permute-start.1 = (bf16[1,196,768]{2,1,0:T(8,128)(2,1)}, bf16[1,196,768]{2,1,0:T(8,128)(2,1)S(1)}, u32[]{:S(2)}, u32[]{:S(2)}) collective-permute-start(bf16[1,196,768]{2,1,0:T(8,128)(2,1)} %param.9), channel_id=1, source_target_pairs={{0,1},{1,2},{2,3},{3,4},{4,5},{5,6},{6,7},{7,8},{8,9},{9,10},{10,1... | collective-permute-start | bytes 903176 | tf_op jit(solution)/shard_map/ppermute | solution.py:18
  5.5 15.8 %collective-permute-start = (bf16[1,196,768]{2,1,0:T(8,128)(2,1)}, bf16[1,196,768]{2,1,0:T(8,128)(2,1)S(1)}, u32[]{:S(2)}, u32[]{:S(2)}) collective-permute-start(bf16[1,196,768]{2,1,0:T(8,128)(2,1)} %param.9), channel_id=1, source_target_pairs={{0,2},{1,3},{2,4},{3,5},{4,6},{5,7},{6,8},{7,9},{8,10},{9,11},{10,... | collective-permute-start | bytes 903176 | tf_op jit(solution)/shard_map/ppermute | solution.py:18
  5.5 19.0 %collective-permute-start.3 = (bf16[1,196,768]{2,1,0:T(8,128)(2,1)}, bf16[1,196,768]{2,1,0:T(8,128)(2,1)S(1)}, u32[]{:S(2)}, u32[]{:S(2)}) collective-permute-start(bf16[1,196,768]{2,1,0:T(8,128)(2,1)} %param.9), channel_id=1, source_target_pairs={{0,14},{1,15},{2,0},{3,1},{4,2},{5,3},{6,4},{7,5},{8,6},{9,7},{10,... | collective-permute-start | bytes 903176 | tf_op jit(solution)/shard_map/ppermute | solution.py:18
  24.5 1.2 copy-start.2
  25.7 2.8 %copy-start.5 = (f32[768]{0:T(1024)S(1)}, f32[768]{0:T(1024)}, u32[]{:S(2)}) copy-start(f32[768]{0:T(1024)} %param.12) | copy-start | bytes 9220
  32.5 3.4 %copy-start.1 = (f32[4,196,1536]{2,1,0:T(8,128)}, f32[4,196,1536]{2,1,0:T(8,128)S(1)}, u32[]{:S(2)}) copy-start(f32[4,196,1536]{2,1,0:T(8,128)S(1)} %fusion.14) | copy-start | bytes 14450692
  80.5 4.2 %copy-start.4 = (bf16[4,196,768]{1,2,0:T(8,128)(2,1)S(1)}, bf16[4,196,768]{1,2,0:T(8,128)(2,1)}, u32[]{:S(2)}) copy-start(bf16[4,196,768]{1,2,0:T(8,128)(2,1)} %copy.29) | copy-start | bytes 3612676
  84.7 2.4 %copy-start.6 = (bf16[768,768]{1,0:T(8,128)(2,1)S(1)}, bf16[768,768]{1,0:T(8,128)(2,1)}, u32[]{:S(2)}) copy-start(bf16[768,768]{1,0:T(8,128)(2,1)} %param.11) | copy-start | bytes 3538948
  88.4 0.7 copy-start.7
  88.4 0.7 copy-start.8
  90.7 3.7 %copy-start.3 = (bf16[4,196,1024]{2,1,0:T(8,128)(2,1)}, bf16[4,196,1024]{2,1,0:T(8,128)(2,1)S(1)}, u32[]{:S(2)}) copy-start(bf16[4,196,1024]{2,1,0:T(8,128)(2,1)S(1)} %add_convert_fusion) | copy-start | bytes 4816900
  94.4 30.2 %collective-permute-start.8 = (bf16[1,196,256]{2,0,1:T(2,128)(2,1)}, bf16[1,196,256]{2,0,1:T(2,128)(2,1)}, u32[]{:S(2)}, u32[]{:S(2)}) collective-permute-start(bf16[1,196,256]{2,0,1:T(2,128)(2,1)} %get-tuple-element.9), channel_id=1, source_target_pairs={{0,14},{1,15},{2,0},{3,1},{4,2},{5,3},{6,4},{7,5},{8,6},{9,7},{10,... | collective-permute-start | bytes 301064 | tf_op jit(solution)/shard_map/ppermute | solution.py:18
  97.8 26.8 %collective-permute-start.11 = (bf16[1,196,256]{2,0,1:T(2,128)(2,1)}, bf16[1,196,256]{2,0,1:T(2,128)(2,1)}, u32[]{:S(2)}, u32[]{:S(2)}) collective-permute-start(bf16[1,196,256]{2,0,1:T(2,128)(2,1)} %get-tuple-element.10), channel_id=1, source_target_pairs={{0,2},{1,3},{2,4},{3,5},{4,6},{5,7},{6,8},{7,9},{8,10},{9,11},{10,... | collective-permute-start | bytes 301064 | tf_op jit(solution)/shard_map/ppermute | solution.py:18
  97.8 26.9 %collective-permute-start.10 = (bf16[1,196,256]{2,0,1:T(2,128)(2,1)}, bf16[1,196,256]{2,0,1:T(2,128)(2,1)}, u32[]{:S(2)}, u32[]{:S(2)}) collective-permute-start(bf16[1,196,256]{2,0,1:T(2,128)(2,1)} %get-tuple-element.11), channel_id=1, source_target_pairs={{0,1},{1,2},{2,3},{3,4},{4,5},{5,6},{6,7},{7,8},{8,9},{9,10},{10,1... | collective-permute-start | bytes 301064 | tf_op jit(solution)/shard_map/ppermute | solution.py:18
  99.6 29.8 %collective-permute-start.9 = (bf16[1,196,256]{2,0,1:T(2,128)(2,1)}, bf16[1,196,256]{2,0,1:T(2,128)(2,1)}, u32[]{:S(2)}, u32[]{:S(2)}) collective-permute-start(bf16[1,196,256]{2,0,1:T(2,128)(2,1)} %get-tuple-element.12), channel_id=1, source_target_pairs={{0,15},{1,0},{2,1},{3,2},{4,3},{5,4},{6,5},{7,6},{8,7},{9,8},{10,9... | collective-permute-start | bytes 301064 | tf_op jit(solution)/shard_map/ppermute | solution.py:18
  124.1 8.2 %collective-permute-start.5 = (bf16[1,196,768]{2,1,0:T(8,128)(2,1)}, bf16[1,196,768]{2,1,0:T(8,128)(2,1)}, u32[]{:S(2)}, u32[]{:S(2)}) collective-permute-start(bf16[1,196,768]{2,1,0:T(8,128)(2,1)} %copy.41), channel_id=1, source_target_pairs={{0,15},{1,0},{2,1},{3,2},{4,3},{5,4},{6,5},{7,6},{8,7},{9,8},{10,9... | collective-permute-start | bytes 903176 | tf_op jit(solution)/shard_map/ppermute | solution.py:18
  124.6 12.0 %collective-permute-start.6 = (bf16[1,196,768]{2,1,0:T(8,128)(2,1)}, bf16[1,196,768]{2,1,0:T(8,128)(2,1)}, u32[]{:S(2)}, u32[]{:S(2)}) collective-permute-start(bf16[1,196,768]{2,1,0:T(8,128)(2,1)} %copy.43), channel_id=1, source_target_pairs={{0,1},{1,2},{2,3},{3,4},{4,5},{5,6},{6,7},{7,8},{8,9},{9,10},{10,1... | collective-permute-start | bytes 903176 | tf_op jit(solution)/shard_map/ppermute | solution.py:18
  124.6 14.0 %collective-permute-start.7 = (bf16[1,196,768]{2,1,0:T(8,128)(2,1)}, bf16[1,196,768]{2,1,0:T(8,128)(2,1)}, u32[]{:S(2)}, u32[]{:S(2)}) collective-permute-start(bf16[1,196,768]{2,1,0:T(8,128)(2,1)} %copy.45), channel_id=1, source_target_pairs={{0,2},{1,3},{2,4},{3,5},{4,6},{5,7},{6,8},{7,9},{8,10},{9,11},{10,... | collective-permute-start | bytes 903176 | tf_op jit(solution)/shard_map/ppermute | solution.py:18
  124.7 19.4 %collective-permute-start.4 = (bf16[1,196,768]{2,1,0:T(8,128)(2,1)S(1)}, bf16[1,196,768]{2,1,0:T(8,128)(2,1)}, u32[]{:S(2)}, u32[]{:S(2)}) collective-permute-start(bf16[1,196,768]{2,1,0:T(8,128)(2,1)S(1)} %copy.39), channel_id=1, source_target_pairs={{0,14},{1,15},{2,0},{3,1},{4,2},{5,3},{6,4},{7,5},{8,6},{9,7},{10,... | collective-permute-start | bytes 903176 | tf_op jit(solution)/shard_map/ppermute | solution.py:18
where the time goes:
time: 149 us
  local copies, waits for them, and re-layouts  48.4 us (32%)
  matrix products  27.2 us (18%)
  other arithmetic  25.7 us (17%)
  starting transfers between devices  24.7 us (17%)
  waiting for transfers between devices  22.2 us (15%)
    ppermute x12, starting transfers between devices, shifted(): return lax.ppermute(value, axis, pairs)  24.7 us
    ppermute x12, waiting for transfers between devices, shifted(): return lax.ppermute(value, axis, pairs)  22.2 us
    mul x4, local copies, waits for them, and re-layouts, head_unit(): return (shaped * lax.rsqrt(energy + EPSILON)).reshape(values.shape)  10.5 us
    mul x2, local copies, waits for them, and re-layouts, contributions(): weight[:, :, None, :]  7.05 us
    dot_general x1, matrix products, contributions(): jnp.einsum('iv,vtx->itx', onehot, weighted, precision=lax.Precision.HIGHEST)  7.01 us
    mul x2, local copies, waits for them, and re-layouts, head_unit(): energy = jnp.mean(shaped * shaped, axis=-1, keepdims=True)  6.79 us
    dot_general x1, matrix products, queries_of(): jnp.einsum('vtd,de->vte', normed, weight_cols, preferred_element_type=jnp...  4.78 us
    reduce_sum x2, other arithmetic, head_unit(): energy = jnp.mean(shaped * shaped, axis=-1, keepdims=True)  4.55 us
  transfers between devices with their start and end apart: 12, of which 5 were waited for; matrix products, arithmetic and copies ran while one was open for 18% of the time, Pallas kernels for 0%

commit v1 on v0

v1 whole, which is shorter than its diff:
```python
import functools

import jax
import jax.numpy as jnp
from jax import lax
from jax.experimental import pallas as pl
from jax.experimental.pallas import tpu as pltpu
from jax.sharding import PartitionSpec as P

HEADS = 12
TEMPER = 16.0
CONF_RANGE = 4.0
EPSILON = 1e-06
LANES = 128
MXU = 256

VMEM_SPEC = pl.BlockSpec(memory_space=pltpu.VMEM)
SMEM_SPEC = pl.BlockSpec(memory_space=pltpu.SMEM)


def round_up(value, step):
    return -(-value // step) * step


def layer_norm(values, gain_row):
    centred = values - jnp.mean(values, axis=-1, keepdims=True)
    spread = jnp.mean(centred * centred, axis=-1, keepdims=True)
    return centred * lax.rsqrt(spread + EPSILON) * gain_row


def matmul(left, right):
    return jnp.dot(left, right, preferred_element_type=jnp.float32)


def head_block(head_size):
    rows = lax.broadcasted_iota(jnp.int32, (MXU, MXU), 0) // head_size
    cols = lax.broadcasted_iota(jnp.int32, (MXU, MXU), 1) // head_size
    return jnp.where(rows == cols, 1.0 / head_size, 0.0).astype(jnp.bfloat16)


def head_unit(mixed, block):
    energy = matmul((mixed * mixed).astype(jnp.bfloat16), block)
    return (mixed * lax.rsqrt(energy + EPSILON)).astype(jnp.bfloat16)


def multiplicity(pair_list, pair_count, own, partner, slots):
    count = jnp.int32(0)
    for slot in range(slots):
        for first, second in ((own, partner), (partner, own)):
            live = slot < pair_count[first]
            hit = pair_list[first * slots + slot, 1] == second
            count = count + jnp.where(jnp.logical_and(live, hit), 1, 0)
    return count


def views_kernel(kinds, first, last, scene_size, slots, *refs):
    refs = list(refs)
    pair_list, pair_count, own_ref = refs[:3]
    partners = refs[3 : 3 + len(kinds)]
    refs = refs[3 + len(kinds) :]
    qkv_ref, out_ref, attn_gain_ref, head_gain_ref, head_ref, bias_ref = refs[:6]
    refs = refs[6:]
    if first:
        q_ref, sums_ref, weights_ref = refs[:3]
        refs = refs[3:]
    else:
        q_ref, sums_in, weights_in = refs[:3]
        refs = refs[3:]
        if last:
            joined_ref = refs[0]
            refs = refs[1:]
            sums_ref, weights_ref = refs[:2]
        else:
            sums_ref, weights_ref = refs[:2]
        refs = refs[2:]
    keys_scr, vals_scr, att_scr = refs
    tokens, width = own_ref.shape
    pixels = head_ref.shape[1] // 4
    head_size = width // HEADS
    rows = q_ref.shape[1] // 2
    padded = keys_scr.shape[0]
    pairs = width // LANES

    position = lax.axis_index("scene")
    parity = lax.rem(position, 2)
    step_to_mate = 1 - 2 * parity
    offsets = {"mate": step_to_mate, "left": -2, "right": 2, "cross": -step_to_mate}
    lane = lax.broadcasted_iota(jnp.int32, (1, LANES), 1)
    low_head = lane < head_size
    block = head_block(head_size)

    keys_scr[...] = jnp.zeros_like(keys_scr)
    row = lax.broadcasted_iota(jnp.int32, (padded, MXU), 0)
    col = lax.broadcasted_iota(jnp.int32, (padded, MXU), 1)
    ones = jnp.where(jnp.logical_and(row < tokens, col >= LANES), 1.0, 0.0).astype(jnp.bfloat16)
    for pair in range(pairs):
        vals_scr[pair] = ones

    if first:
        normed = layer_norm(own_ref[...].astype(jnp.float32), attn_gain_ref[...]).astype(jnp.bfloat16)
        q_ref[...] = jnp.zeros_like(q_ref)
        for start in range(0, width, MXU):
            unit = head_unit(matmul(normed, qkv_ref[:, start : start + MXU]), block)
            for half in range(MXU // LANES):
                pair = start // LANES + half
                piece = unit[:, half * LANES : (half + 1) * LANES]
                zero = jnp.zeros_like(piece)
                q_ref[pair, :tokens, :] = jnp.where(low_head, piece, zero)
                q_ref[pair, rows : rows + tokens, :] = jnp.where(low_head, zero, piece)
        sums_ref[...] = jnp.zeros_like(sums_ref)
        weights_ref[...] = jnp.zeros_like(weights_ref)
    else:
        sums_ref[...] = sums_in[...]
        weights_ref[...] = weights_in[...]

    for kind, partner_ref in zip(kinds, partners):
        partner = lax.rem(position + offsets[kind] + scene_size, scene_size)
        count = multiplicity(pair_list, pair_count, position, partner, slots)

        @pl.when(count > 0)
        def _():
            normed = layer_norm(partner_ref[...].astype(jnp.float32), attn_gain_ref[...]).astype(jnp.bfloat16)
            for start in range(0, width, MXU):
                keys_scr[:tokens, start : start + MXU] = head_unit(
                    matmul(normed, qkv_ref[:, width + start : width + start + MXU]), block
                )
                value = matmul(normed, qkv_ref[:, 2 * width + start : 2 * width + start + MXU]).astype(jnp.bfloat16)
                for half in range(MXU // LANES):
                    vals_scr[start // LANES + half, :tokens, :LANES] = value[:, half * LANES : (half + 1) * LANES]
            for pair in range(pairs):
                scores = lax.dot_general(
                    q_ref[pair],
                    keys_scr[:, pair * LANES : (pair + 1) * LANES],
                    (((1,), (1,)), ((), ())),
                    preferred_element_type=jnp.float32,
                )
                exponent = jnp.exp(scores * (TEMPER / head_size)).astype(jnp.bfloat16)
                mixed = matmul(exponent, vals_scr[pair])
                top = jnp.where(low_head, mixed[:tokens, :LANES], mixed[rows : rows + tokens, :LANES])
                norm = jnp.where(low_head, mixed[:tokens, LANES:], mixed[rows : rows + tokens, LANES:])
                att_scr[:, pair * LANES : (pair + 1) * LANES] = (top / norm).astype(jnp.bfloat16)
            mixed = own_ref[...].astype(jnp.float32) + matmul(att_scr[...], out_ref[...])
            head_in = layer_norm(mixed, head_gain_ref[...]).astype(jnp.bfloat16)
            conf = matmul(head_in, head_ref[:, 3 * pixels :]) + bias_ref[:, 3 * pixels :]
            conf = conf.astype(jnp.bfloat16).astype(jnp.float32)
            weight = jnp.exp(CONF_RANGE * jnp.tanh(conf / CONF_RANGE)) * count.astype(jnp.float32)
            weights_ref[...] += weight
            for part in range(3):
                cols = slice(part * pixels, (part + 1) * pixels)
                xyz = matmul(head_in, head_ref[:, cols]) + bias_ref[:, cols]
                sums_ref[:, cols] += weight * xyz.astype(jnp.bfloat16).astype(jnp.float32)

    if last:
        for part in range(3):
            cols = slice(part * pixels, (part + 1) * pixels)
            joined_ref[:, cols] = sums_ref[:, cols] / weights_ref[...]


def run_views(kinds, first, last, scene_size, pair_list, pair_count, own, partners, params, state):
    tokens, width = own.shape
    slots = pair_list.shape[0] // scene_size
    pixels = params[4].shape[1] // 4
    rows = round_up(tokens, 16)
    padded = round_up(tokens, MXU)
    pairs = width // LANES
    f32, bf16 = jnp.float32, jnp.bfloat16
    sums = jax.ShapeDtypeStruct((tokens, 3 * pixels), f32)
    weights = jax.ShapeDtypeStruct((tokens, pixels), f32)
    scratch = []
    if first:
        out_shape = (jax.ShapeDtypeStruct((pairs, 2 * rows, LANES), bf16), sums, weights)
    elif last:
        out_shape = jax.ShapeDtypeStruct((tokens, 3 * pixels), f32)
        scratch = [pltpu.VMEM(sums.shape, f32), pltpu.VMEM(weights.shape, f32)]
    else:
        out_shape = (sums, weights)
    scratch += [
        pltpu.VMEM((padded, width), bf16),
        pltpu.VMEM((pairs, padded, MXU), bf16),
        pltpu.VMEM((tokens, width), bf16),
    ]
    operands = [pair_list, pair_count, own, *partners, *params, *state]
    return pl.pallas_call(
        functools.partial(views_kernel, kinds, first, last, scene_size, slots),
        out_shape=out_shape,
        in_specs=[SMEM_SPEC, SMEM_SPEC] + [VMEM_SPEC] * (len(operands) - 2),
        out_specs=jax.tree.map(lambda _: VMEM_SPEC, out_shape),
        scratch_shapes=scratch,
        compiler_params=pltpu.CompilerParams(vmem_limit_bytes=24 * 2**20),
        cost_estimate=pl.CostEstimate(
            flops=len(kinds) * 4 * tokens * width * width * 2, bytes_accessed=8 * 2**20, transcendentals=0
        ),
        name="views_" + "_".join(kinds),
    )(*operands)


def per_device(
    tokens, qkv_weight, out_weight, attn_gain, head_gain, head_weight, head_bias, pair_list, pair_count
):
    scene_size = lax.axis_size("scene")
    own = tokens[0]
    params = (
        qkv_weight,
        out_weight,
        attn_gain.reshape(1, -1),
        head_gain.reshape(1, -1),
        head_weight,
        head_bias.reshape(1, -1),
    )

    def moved(value, target_of):
        return lax.ppermute(value, "scene", [(s, target_of(s)) for s in range(scene_size)])

    mate = moved(own, lambda s: s ^ 1)
    left = moved(own, lambda s: (s + 2) % scene_size)
    right = moved(own, lambda s: (s - 2) % scene_size)
    views = functools.partial(run_views, scene_size=scene_size, pair_list=pair_list, pair_count=pair_count, own=own, params=params)
    queries, sums, weights = views(("mate",), True, False, partners=(mate,), state=())
    parity = lax.rem(lax.axis_index("scene"), 2)
    cross = moved(jnp.where(parity == 0, right, left), lambda s: s ^ 1)
    sums, weights = views(("left", "right"), False, False, partners=(left, right), state=(queries, sums, weights))
    joined = views(("cross",), False, True, partners=(cross,), state=(queries, sums, weights))
    return joined[None]


def solution(mesh):
    return jax.shard_map(
        per_device,
        mesh=mesh,
        in_specs=(
            P(("groups", "scene"), None, None),
            P(),
            P(),
            P(),
            P(),
            P(),
            P(),
            P("groups", None),
            P("groups"),
        ),
        out_specs=P(("groups", "scene"), None, None),
        check_vma=False,
    )
```

time: 149 us -> 44 us (0.30)
  local copies, waits for them, and re-layouts: 48.4 us -> 10.6 us
  matrix products: 27.2 us -> 0 us
  other arithmetic: 25.7 us -> 0.03 us
  starting transfers between devices: 24.7 us -> 6.11 us
  Pallas kernels: 0 us -> 15.8 us
  waiting for transfers between devices: 22.2 us -> 11.6 us
    dot_general x8 -> x0, matrix products: 27.2 us -> none  [the longest x1 7.01 us: contributions(): jnp.einsum('iv,vtx->itx', onehot, weighted, precision=lax.Precision.HIGHEST)]
    mul x8 -> x0, local copies, waits for them, and re-layouts: 24.4 us -> none  [the longest x4 10.5 us: head_unit(): return (shaped * lax.rsqrt(energy + EPSILON)).reshape(values.shape)]
    ppermute x12 -> x4, starting transfers between devices: 24.7 us -> 6.11 us  [moved(): lax.ppermute(value, 'scene', [(s, target_of(s)) for s in range(scene_size)])]
    pallas_call x0 -> x3, Pallas kernels: none -> 15.8 us  [run_views(): pl.pallas_call(functools.partial(views_kernel, kinds, first, last, scene_...]
    ppermute x12 -> x4, waiting for transfers between devices: 22.2 us -> 11.6 us  [moved(): lax.ppermute(value, 'scene', [(s, target_of(s)) for s in range(scene_size)])]
    slice x8 -> x0, local copies, waits for them, and re-layouts: 9.39 us -> none  [the longest x5 4.07 us: per_device(): window_sum[row_start:row_start + image_count].astype(jnp.bfloat16)]
    convert_element_type x2 -> x0, other arithmetic: 7.42 us -> none  [the longest x1 3.71 us: keys_values_of(): head_unit(mixed[..., :model_width]).astype(jnp.bfloat16)]
    reduce_sum x7 -> x0, other arithmetic: 6.5 us -> none  [the longest x2 4.55 us: head_unit(): energy = jnp.mean(shaped * shaped, axis=-1, keepdims=True)]
  transfers between devices with their start and end apart: 12 -> 4, of which waited for: 5 -> 2; matrix products, arithmetic and copies ran while one was open for 18% -> 5% of each run, Pallas kernels for 0% -> 27%
where the time goes in v1:
time: 44 us; the launch traced here: 44.2 us
  Pallas kernels  15.8 us (36%)
  waiting for transfers between devices  11.6 us (26%)
  local copies, waits for them, and re-layouts  10.6 us (24%)
  starting transfers between devices  6.11 us (14%)
    pallas_call x3, Pallas kernels, run_views(): pl.pallas_call(functools.partial(views_kernel, kinds, first, last, scene_...  15.8 us
    ppermute x4, waiting for transfers between devices, moved(): lax.ppermute(value, 'scene', [(s, target_of(s)) for s in range(scene_size)])  11.6 us
    unnamed x23, local copies, waits for them, and re-layouts  7.77 us
    ppermute x4, starting transfers between devices, moved(): lax.ppermute(value, 'scene', [(s, target_of(s)) for s in range(scene_size)])  6.11 us
    broadcast_in_dim x1, local copies, waits for them, and re-layouts, per_device(): return joined[None]  1.44 us
  transfers between devices with their start and end apart: 4, of which 2 were waited for; matrix products, arithmetic and copies ran while one was open for 5% of the time, Pallas kernels for 27%

profile of v1, /device:TPU:0, one launch (start us, length us, event | category | flops | bytes accessed | tf_op | source)
XLA Modules:
  0.0 44.2 jit_solution(15413155437537605122)
XLA Ops:
  0.0 6.0 %collective-permute-start = (bf16[196,768]{1,0:T(8,128)(2,1)}, bf16[196,768]{1,0:T(8,128)(2,1)S(1)}, u32[]{:S(2)}, u32[]{:S(2)}) collective-permute-start(bf16[196,768]{1,0:T(8,128)(2,1)} %bitcast.3), channel_id=1, source_target_pairs={{0,14},{1,15},{2,0},{3,1},{4,2},{5,3},{6,4},{7,5},{8,6},{9,7},{10,... | collective-permute-start | bytes 903176 | tf_op jit(solution)/shard_map/ppermute | solution.py:212
  6.0 0.0 collective-permute-start.1
  6.0 0.0 collective-permute-start.3
  6.0 6.8 %collective-permute-done.refs_4_ = bf16[196,768]{1,0:T(8,128)(2,1)S(1)} collective-permute-done((bf16[196,768]{1,0:T(8,128)(2,1)}, bf16[196,768]{1,0:T(8,128)(2,1)S(1)}, u32[]{:S(2)}, u32[]{:S(2)}) %collective-permute-start) | collective-permute-done | bytes 301088 | tf_op jit(solution)/shard_map/ppermute | solution.py:212
  12.9 4.8 %collective-permute-done.1.refs_3_ = bf16[196,768]{1,0:T(8,128)(2,1)S(1)} collective-permute-done((bf16[196,768]{1,0:T(8,128)(2,1)}, bf16[196,768]{1,0:T(8,128)(2,1)S(1)}, u32[]{:S(2)}, u32[]{:S(2)}) %collective-permute-start.1) | collective-permute-done | bytes 301088 | tf_op jit(solution)/shard_map/ppermute | solution.py:212
  17.7 0.1 collective-permute-start.2
  17.8 0.8 %copy.12.refs_0_ = s32[32,2]{1,0:T(8,128)S(1)} copy(s32[32,2]{0,1:T(2,128)} %param.16) | data formatting | bytes 512 | tf_op args[7]
  18.6 0.7 %reshape.10.refs_7_.refs_8_ = f32[1,768]{1,0:T(1,128)S(1)} reshape(f32[768]{0:T(1024)} %param.13) | data formatting | bytes 6144 | tf_op jit(solution)/shard_map/reshape | solution.py:206
  19.2 0.7 %reshape.9.refs_6_.refs_7_ = f32[1,768]{1,0:T(1,128)S(1)} reshape(f32[768]{0:T(1024)} %param.12) | data formatting | bytes 6144 | tf_op jit(solution)/shard_map/reshape | solution.py:205
  19.9 0.0 collective-permute-done.3.refs_3_
  19.9 0.0 copy-start
  19.9 2.0 %copy-done = bf16[768,2304]{1,0:T(8,128)(2,1)S(1)} copy-done((bf16[768,2304]{1,0:T(8,128)(2,1)S(1)}, bf16[768,2304]{1,0:T(8,128)(2,1)}, u32[]{:S(2)}) %copy-start) | copy-done | bytes 3538968
  21.9 0.0 copy-start.2
  21.9 1.4 %copy-done.2 = bf16[768,1024]{1,0:T(8,128)(2,1)S(1)} copy-done((bf16[768,1024]{1,0:T(8,128)(2,1)S(1)}, bf16[768,1024]{1,0:T(8,128)(2,1)}, u32[]{:S(2)}) %copy-start.2) | copy-done | bytes 1572888
  23.3 0.0 copy-start.4
  23.3 1.3 %copy-done.4 = bf16[768,768]{1,0:T(8,128)(2,1)S(1)} copy-done((bf16[768,768]{1,0:T(8,128)(2,1)S(1)}, bf16[768,768]{1,0:T(8,128)(2,1)}, u32[]{:S(2)}) %copy-start.4) | copy-done | bytes 1179672
  24.6 0.0 copy-start.6
  24.6 1.0 %copy-done.6 = bf16[1,196,768]{2,1,0:T(8,128)(2,1)S(1)} copy-done((bf16[1,196,768]{2,1,0:T(8,128)(2,1)S(1)}, bf16[1,196,768]{2,1,0:T(8,128)(2,1)}, u32[]{:S(2)}) %copy-start.6) | copy-done | bytes 301080
  25.6 0.0 copy-start.7
  25.6 0.7 %copy-done.7 = f32[1024]{0:T(1024)S(1)} copy-done((f32[1024]{0:T(1024)S(1)}, f32[1024]{0:T(1024)}, u32[]{:S(2)}) %copy-start.7) | copy-done | bytes 4120
  26.3 0.0 copy-start.9
  26.3 0.7 %copy-done.9 = s32[16]{0:T(128)S(1)} copy-done((s32[16]{0:T(128)S(1)}, s32[16]{0:T(128)}, u32[]{:S(2)}) %copy-start.9) | copy-done | bytes 88
  26.9 0.0 copy-start.1
  26.9 0.0 copy-start.3
  26.9 0.0 copy-start.5
  26.9 0.0 copy-start.10
  26.9 5.1 %views_mate.1 = (bf16[6,416,128]{2,1,0:T(8,128)(2,1)S(1)}, f32[196,768]{1,0:T(8,128)S(1)}, f32[196,256]{1,0:T(8,128)S(1)}) custom-call(s32[32,2]{1,0:T(8,128)S(1)} %copy.12.refs_0_, s32[16]{0:T(128)S(1)} %copy-done.9, bf16[196,768]{1,0:T(8,128)(2,1)S(1)} %bitcast.6, bf16[196,768]{1,0:T(8,128)(2,1)S(1)} %collective-permute-done.3.refs_3_, ...), custom_call_target="tpu_custom_call" | custom-call | flops 924844032 | bytes 8388608 | tf_op jit(solution)/shard_map/views_mate/pallas_call | solution.py:183
  32.0 0.0 copy-done.1
  32.0 0.0 copy-done.3
  32.0 0.0 copy-done.5
  32.0 0.0 copy-done.10
  32.0 0.0 copy-start.8
  32.1 6.8 %views_left_right.1 = (f32[196,768]{1,0:T(8,128)S(1)}, f32[196,256]{1,0:T(8,128)S(1)}) custom-call(s32[32,2]{1,0:T(8,128)S(1)} %copy.12.refs_0_, s32[16]{0:T(128)S(1)} %copy-done.10, bf16[196,768]{1,0:T(8,128)(2,1)S(1)} %bitcast.7, bf16[196,768]{1,0:T(8,128)(2,1)S(1)} %collective-permute-done.1.refs_3_, bf16[196,768]{1,0:T(8,128)(2,1)S(1)} %collective-permute-done.refs_4_, ...), custom_call_target="tpu_custom_call" | custom-call | flops 1849688064 | bytes 8388608 | tf_op jit(solution)/shard_map/views_left_right/pallas_call | solution.py:183
  38.9 0.0 collective-permute-done.2.refs_3_
  38.9 0.0 copy-done.8
  38.9 3.9 %views_cross.1 = f32[196,768]{1,0:T(8,128)S(1)} custom-call(s32[32,2]{1,0:T(8,128)S(1)} %copy.12.refs_0_, s32[16]{0:T(128)S(1)} %copy-done.10, bf16[196,768]{1,0:T(8,128)(2,1)S(1)} %bitcast.8, bf16[196,768]{1,0:T(8,128)(2,1)S(1)} %collective-permute-done.2.refs_3_, bf16[768,2304]{1,0:T(8,128)(2,1)S(1)} %copy-done.1, bf16[768,768]{1,0:T(8,128)(2,1)S(1)} %copy-done.5, ...), custom_call_target="tpu_custom_call" | custom-call | flops 924844032 | bytes 8388608 | tf_op jit(solution)/shard_map/views_cross/pallas_call | solution.py:183
  42.8 1.4 %copy.13 = f32[1,196,768]{2,0,1:T(1,128)} copy(f32[1,196,768]{2,1,0:T(8,128)S(1)} %bitcast.9) | data formatting | bytes 1204224 | tf_op jit(solution)/shard_map/broadcast_in_dim | solution.py:223
  (1 shorter events, 0.0 us)
Async XLA Ops:
  0.0 12.9 %collective-permute-start = (bf16[196,768]{1,0:T(8,128)(2,1)}, bf16[196,768]{1,0:T(8,128)(2,1)S(1)}, u32[]{:S(2)}, u32[]{:S(2)}) collective-permute-start(bf16[196,768]{1,0:T(8,128)(2,1)} %bitcast.3), channel_id=1, source_target_pairs={{0,14},{1,15},{2,0},{3,1},{4,2},{5,3},{6,4},{7,5},{8,6},{9,7},{10,... | collective-permute-start | bytes 903176 | tf_op jit(solution)/shard_map/ppermute | solution.py:212
  6.0 11.6 %collective-permute-start.1 = (bf16[196,768]{1,0:T(8,128)(2,1)}, bf16[196,768]{1,0:T(8,128)(2,1)S(1)}, u32[]{:S(2)}, u32[]{:S(2)}) collective-permute-start(bf16[196,768]{1,0:T(8,128)(2,1)} %bitcast.4), channel_id=1, source_target_pairs={{0,2},{1,3},{2,4},{3,5},{4,6},{5,7},{6,8},{7,9},{8,10},{9,11},{10,... | collective-permute-start | bytes 903176 | tf_op jit(solution)/shard_map/ppermute | solution.py:212
  6.0 13.9 %collective-permute-start.3 = (bf16[196,768]{1,0:T(8,128)(2,1)}, bf16[196,768]{1,0:T(8,128)(2,1)S(1)}, u32[]{:S(2)}, u32[]{:S(2)}) collective-permute-start(bf16[196,768]{1,0:T(8,128)(2,1)} %bitcast.5), channel_id=1, source_target_pairs={{0,1},{1,0},{2,3},{3,2},{4,5},{5,4},{6,7},{7,6},{8,9},{9,8},{10,11... | collective-permute-start | bytes 903176 | tf_op jit(solution)/shard_map/ppermute | solution.py:212
  17.7 21.1 %collective-permute-start.2 = (bf16[196,768]{1,0:T(8,128)(2,1)S(1)}, bf16[196,768]{1,0:T(8,128)(2,1)S(1)}, u32[]{:S(2)}, u32[]{:S(2)}) collective-permute-start(bf16[196,768]{1,0:T(8,128)(2,1)S(1)} %broadcast_select_fusion), channel_id=1, source_target_pairs={{0,1},{1,0},{2,3},{3,2},{4,5},{5,4},{6,7},{7,6},{8,9},{9,8},{10,11... | collective-permute-start | bytes 903176 | tf_op jit(solution)/shard_map/ppermute | solution.py:212
  19.9 2.0 %copy-start = (bf16[768,2304]{1,0:T(8,128)(2,1)S(1)}, bf16[768,2304]{1,0:T(8,128)(2,1)}, u32[]{:S(2)}) copy-start(bf16[768,2304]{1,0:T(8,128)(2,1)} %refs_4_.3) | copy-start | bytes 10616836
  21.9 1.4 %copy-start.2 = (bf16[768,1024]{1,0:T(8,128)(2,1)S(1)}, bf16[768,1024]{1,0:T(8,128)(2,1)}, u32[]{:S(2)}) copy-start(bf16[768,1024]{1,0:T(8,128)(2,1)} %refs_8_.3) | copy-start | bytes 4718596
  23.3 1.3 %copy-start.4 = (bf16[768,768]{1,0:T(8,128)(2,1)S(1)}, bf16[768,768]{1,0:T(8,128)(2,1)}, u32[]{:S(2)}) copy-start(bf16[768,768]{1,0:T(8,128)(2,1)} %refs_5_.5) | copy-start | bytes 3538948
  24.6 1.0 %copy-start.6 = (bf16[1,196,768]{2,1,0:T(8,128)(2,1)S(1)}, bf16[1,196,768]{2,1,0:T(8,128)(2,1)}, u32[]{:S(2)}) copy-start(bf16[1,196,768]{2,1,0:T(8,128)(2,1)} %param.9) | copy-start | bytes 903172
  25.6 0.7 %copy-start.7 = (f32[1024]{0:T(1024)S(1)}, f32[1024]{0:T(1024)}, u32[]{:S(2)}) copy-start(f32[1024]{0:T(1024)} %param.15) | copy-start | bytes 12292
  26.3 0.7 %copy-start.9 = (s32[16]{0:T(128)S(1)}, s32[16]{0:T(128)}, u32[]{:S(2)}) copy-start(s32[16]{0:T(128)} %refs_1_.5) | copy-start | bytes 196
  26.9 5.1 %copy-start.1 = (bf16[768,2304]{1,0:T(8,128)(2,1)S(1)}, bf16[768,2304]{1,0:T(8,128)(2,1)}, u32[]{:S(2)}) copy-start(bf16[768,2304]{1,0:T(8,128)(2,1)} %refs_4_.3) | copy-start | bytes 10616836
  26.9 5.1 %copy-start.3 = (bf16[768,1024]{1,0:T(8,128)(2,1)S(1)}, bf16[768,1024]{1,0:T(8,128)(2,1)}, u32[]{:S(2)}) copy-start(bf16[768,1024]{1,0:T(8,128)(2,1)} %refs_8_.3) | copy-start | bytes 4718596
  26.9 5.1 %copy-start.5 = (bf16[768,768]{1,0:T(8,128)(2,1)S(1)}, bf16[768,768]{1,0:T(8,128)(2,1)}, u32[]{:S(2)}) copy-start(bf16[768,768]{1,0:T(8,128)(2,1)} %refs_5_.5) | copy-start | bytes 3538948
  26.9 5.1 %copy-start.10 = (s32[16]{0:T(128)S(1)}, s32[16]{0:T(128)}, u32[]{:S(2)}) copy-start(s32[16]{0:T(128)} %refs_1_.5) | copy-start | bytes 196
  32.0 6.8 %copy-start.8 = (f32[1024]{0:T(1024)S(1)}, f32[1024]{0:T(1024)}, u32[]{:S(2)}) copy-start(f32[1024]{0:T(1024)} %param.15) | copy-start | bytes 12292

commit v2 on v1

v2 whole, which is shorter than its diff:
```python
import functools

import jax
import jax.numpy as jnp
from jax import lax
from jax.experimental import pallas as pl
from jax.experimental.pallas import tpu as pltpu
from jax.sharding import PartitionSpec as P


HEADS = 12
TEMPER = 16.0
CONF_RANGE = 4.0
EPSILON = 1e-06
LANES = 128
MXU = 256

VMEM_SPEC = pl.BlockSpec(memory_space=pltpu.VMEM)
HBM_SPEC = pl.BlockSpec(memory_space=pltpu.HBM)


def in_hbm(value):
    return pltpu.with_memory_space_constraint(value, pltpu.HBM)


def round_up(value, step):
    return -(-value // step) * step


def layer_norm(values, gain_row):
    centred = values - jnp.mean(values, axis=-1, keepdims=True)
    spread = jnp.mean(centred * centred, axis=-1, keepdims=True)
    return centred * lax.rsqrt(spread + EPSILON) * gain_row


def matmul(left, right):
    return jnp.dot(left, right, preferred_element_type=jnp.float32)


def head_block(head_size):
    rows = lax.broadcasted_iota(jnp.int32, (MXU, MXU), 0) // head_size
    cols = lax.broadcasted_iota(jnp.int32, (MXU, MXU), 1) // head_size
    return jnp.where(rows == cols, 1.0 / head_size, 0.0).astype(jnp.bfloat16)


def head_unit(mixed, block):
    energy = matmul((mixed * mixed).astype(jnp.bfloat16), block)
    return (mixed * lax.rsqrt(energy + EPSILON)).astype(jnp.bfloat16)


def multiplicity(pair_list, pair_count, own, partner, slots):
    count = jnp.int32(0)
    for slot in range(slots):
        for first, second in ((own, partner), (partner, own)):
            live = slot < pair_count[first]
            hit = pair_list[1, first * slots + slot] == second
            count = count + jnp.where(jnp.logical_and(live, hit), 1, 0)
    return count


def one_view(partner, count_row, own_ref, q_ref, kv_ref, out_ref, head_ref, gains_ref, bias_ref, keys_scr, vals_scr, att_scr, emit):
    tokens, width = own_ref.shape
    head_size = width // HEADS
    pixels = head_ref.shape[1] // 4
    rows = q_ref.shape[1] // 2
    padded = keys_scr.shape[0]
    pairs = width // LANES
    low_head = lax.broadcasted_iota(jnp.int32, (1, LANES), 1) < head_size
    block = head_block(head_size)

    tail = tokens // 16 * 16
    keys_scr[tail:, :] = jnp.zeros((padded - tail, width), jnp.bfloat16)
    row = lax.broadcasted_iota(jnp.int32, (padded, LANES), 0)
    ones = jnp.where(row < tokens, 1.0, 0.0).astype(jnp.bfloat16)
    for pair in range(pairs):
        vals_scr[pair, tail:, :LANES] = jnp.zeros((padded - tail, LANES), jnp.bfloat16)
        vals_scr[pair, :, LANES:] = ones

    normed = layer_norm(partner.astype(jnp.float32), gains_ref[0:1, :]).astype(jnp.bfloat16)
    for start in range(0, width, MXU):
        keys_scr[:tokens, start : start + MXU] = head_unit(matmul(normed, kv_ref[:, start : start + MXU]), block)
        value = matmul(normed, kv_ref[:, width + start : width + start + MXU]).astype(jnp.bfloat16)
        for half in range(MXU // LANES):
            vals_scr[start // LANES + half, :tokens, :LANES] = value[:, half * LANES : (half + 1) * LANES]
    for pair in range(pairs):
        scores = lax.dot_general(
            q_ref[pair],
            keys_scr[:, pair * LANES : (pair + 1) * LANES],
            (((1,), (1,)), ((), ())),
            preferred_element_type=jnp.float32,
        )
        exponent = jnp.exp(scores * (TEMPER / head_size)).astype(jnp.bfloat16)
        mixed = matmul(exponent, vals_scr[pair])
        top = jnp.where(low_head, mixed[:tokens, :LANES], mixed[rows : rows + tokens, :LANES])
        norm = jnp.where(low_head, mixed[:tokens, LANES:], mixed[rows : rows + tokens, LANES:])
        att_scr[:, pair * LANES : (pair + 1) * LANES] = (top / norm).astype(jnp.bfloat16)
    mixed = own_ref[...].astype(jnp.float32) + matmul(att_scr[...], out_ref[...])
    head_in = layer_norm(mixed, gains_ref[1:2, :]).astype(jnp.bfloat16)
    conf = matmul(head_in, head_ref[:, 3 * pixels :]) + bias_ref[:, 3 * pixels :]
    conf = conf.astype(jnp.bfloat16).astype(jnp.float32)
    weight = jnp.exp(CONF_RANGE * jnp.tanh(conf / CONF_RANGE)) * count_row
    for part in range(3):
        cols = slice(part * pixels, (part + 1) * pixels)
        xyz = matmul(head_in, head_ref[:, cols]) + bias_ref[:, cols]
        emit(part, cols, weight, weight * xyz.astype(jnp.bfloat16).astype(jnp.float32))


def view_scratch(tokens, width):
    padded, pairs = round_up(tokens, MXU), width // LANES
    return [
        pltpu.VMEM((padded, width), jnp.bfloat16),
        pltpu.VMEM((pairs, padded, MXU), jnp.bfloat16),
        pltpu.VMEM((tokens, width), jnp.bfloat16),
    ]


def first_kernel(
    scene_size,
    slots,
    offsets_of,
    tokens_hbm,
    qkv_hbm,
    out_hbm,
    attn_gain_hbm,
    head_gain_hbm,
    head_hbm,
    bias_hbm,
    list_hbm,
    count_hbm,
    own_ref,
    kv_ref,
    out_ref,
    head_ref,
    gains_ref,
    bias_ref,
    counts_ref,
    q_ref,
    wq_scr,
    list_smem,
    count_smem,
    sems,
):
    tokens, width = own_ref.shape
    head_size = width // HEADS
    rows = q_ref.shape[1] // 2
    plan = [
        (tokens_hbm.at[0], own_ref),
        (attn_gain_hbm, gains_ref.at[0]),
        (qkv_hbm.at[:, :width], wq_scr),
        (head_gain_hbm, gains_ref.at[1]),
        (bias_hbm, bias_ref.at[0]),
        (list_hbm, list_smem),
        (count_hbm, count_smem),
        (qkv_hbm.at[:, width : 2 * width], kv_ref.at[:, :width]),
        (qkv_hbm.at[:, 2 * width :], kv_ref.at[:, width:]),
        (out_hbm, out_ref),
        (head_hbm, head_ref),
    ]
    copies = [pltpu.make_async_copy(source, target, sems.at[at]) for at, (source, target) in enumerate(plan)]
    for copy in copies:
        copy.start()
    for copy in copies[:3]:
        copy.wait()
    low_head = lax.broadcasted_iota(jnp.int32, (1, LANES), 1) < head_size
    block = head_block(head_size)
    normed = layer_norm(own_ref[...].astype(jnp.float32), gains_ref[0:1, :]).astype(jnp.bfloat16)
    q_ref[...] = jnp.zeros_like(q_ref)
    for start in range(0, width, MXU):
        unit = head_unit(matmul(normed, wq_scr[:, start : start + MXU]), block)
        for half in range(MXU // LANES):
            pair = start // LANES + half
            piece = unit[:, half * LANES : (half + 1) * LANES]
            zero = jnp.zeros_like(piece)
            q_ref[pair, :tokens, :] = jnp.where(low_head, piece, zero)
            q_ref[pair, rows : rows + tokens, :] = jnp.where(low_head, zero, piece)
    for copy in copies[3:]:
        copy.wait()
    position = lax.axis_index("scene")
    for at, offset in enumerate(offsets_of(position)):
        partner = lax.rem(position + offset + scene_size, scene_size)
        count = multiplicity(list_smem, count_smem, position, partner, slots).astype(jnp.float32)
        counts_ref[at] = jnp.full(counts_ref.shape[1:], count, jnp.float32)


def view_kernel(
    at, first, last, own_ref, kv_ref, out_ref, head_ref, gains_ref, bias_ref, counts_ref, q_ref, partner_ref, *refs
):
    if not first:
        sums_in, weights_in, *refs = refs
    if last:
        joined_hbm, keys_scr, vals_scr, att_scr, joined_scr, sems = refs
    else:
        sums_ref, weights_ref, keys_scr, vals_scr, att_scr = refs
    copies = []

    def emit(part, cols, weight, weighted):
        total = weighted if first else sums_in[:, cols] + weighted
        weight = weight if first else weights_in[...] + weight
        if last:
            joined_scr[:, cols] = total / weight
            copy = pltpu.make_async_copy(joined_scr.at[:, cols], joined_hbm.at[:, 0, cols], sems.at[part])
            copy.start()
            copies.append(copy)
        else:
            sums_ref[:, cols] = total
            if part == 0:
                weights_ref[...] = weight

    one_view(
        partner_ref[...], counts_ref[at, 0:1, 0:1], own_ref, q_ref, kv_ref, out_ref, head_ref, gains_ref, bias_ref,
        keys_scr, vals_scr, att_scr, emit,
    )
    for copy in copies:
        copy.wait()


def per_device(
    tokens, qkv_weight, out_weight, attn_gain, head_gain, head_weight, head_bias, pair_list, pair_count
):
    scene_size = lax.axis_size("scene")
    _, token_count, width = tokens.shape
    slots = pair_list.shape[0] // scene_size
    columns = head_weight.shape[1]
    pixels = columns // 4
    f32, bf16 = jnp.float32, jnp.bfloat16
    own = tokens[0]

    def moved(value, target_of):
        return lax.ppermute(value, "scene", [(s, target_of(s) % scene_size) for s in range(scene_size)])

    def mate_of(s):
        return s ^ 1

    def offsets_of(position):
        to_mate = 1 - 2 * lax.rem(position, 2)
        return (to_mate, -to_mate, 2 * to_mate, -2 * to_mate)

    sums = jax.ShapeDtypeStruct((token_count, 3 * pixels), f32)
    weights = jax.ShapeDtypeStruct((token_count, pixels), f32)
    params = pltpu.CompilerParams(vmem_limit_bytes=24 * 2**20)
    cost = pl.CostEstimate(flops=4 * token_count * width * width * 2, bytes_accessed=2**20, transcendentals=0)

    alpha = moved(own, lambda s: s + 1 if s % 2 else s - 1)
    mate = moved(own, mate_of)
    first_shapes = (
        jax.ShapeDtypeStruct((token_count, width), bf16),
        jax.ShapeDtypeStruct((width, 2 * width), bf16),
        jax.ShapeDtypeStruct(out_weight.shape, bf16),
        jax.ShapeDtypeStruct(head_weight.shape, bf16),
        jax.ShapeDtypeStruct((2, width), f32),
        jax.ShapeDtypeStruct((1, columns), f32),
        jax.ShapeDtypeStruct((4, 8, LANES), f32),
        jax.ShapeDtypeStruct((width // LANES, 2 * round_up(token_count, 16), LANES), bf16),
    )
    state = pl.pallas_call(
        functools.partial(first_kernel, scene_size, slots, offsets_of),
        out_shape=first_shapes,
        in_specs=[HBM_SPEC] * 9,
        out_specs=tuple(VMEM_SPEC for _ in first_shapes),
        scratch_shapes=[
            pltpu.VMEM((width, width), bf16),
            pltpu.SMEM((2, pair_list.shape[0]), jnp.int32),
            pltpu.SMEM(pair_count.shape, jnp.int32),
            pltpu.SemaphoreType.DMA((11,)),
        ],
        compiler_params=params,
        cost_estimate=cost,
        name="load_queries",
    )(
        in_hbm(tokens),
        *(in_hbm(value) for value in (qkv_weight, out_weight, attn_gain, head_gain, head_weight, head_bias)),
        in_hbm(pair_list.T),
        in_hbm(pair_count),
    )

    def view(at, partner, totals, last=False):
        out_shape = jax.ShapeDtypeStruct((token_count, 1, 3 * pixels), f32) if last else (sums, weights)
        scratch = view_scratch(token_count, width)
        if last:
            scratch += [pltpu.VMEM(sums.shape, f32), pltpu.SemaphoreType.DMA((3,))]
        operands = (*state, partner, *totals)
        return pl.pallas_call(
            functools.partial(view_kernel, at, not totals, last),
            out_shape=out_shape,
            in_specs=[VMEM_SPEC] * len(operands),
            out_specs=HBM_SPEC if last else (VMEM_SPEC, VMEM_SPEC),
            scratch_shapes=scratch,
            compiler_params=params,
            cost_estimate=cost,
        )(*operands)

    own, queries = lax.optimization_barrier((own, state[-1]))
    state = (*state[:-1], queries)
    beta = moved(own, lambda s: s - 2 if s % 2 else s + 2)
    totals = view(0, mate, ())
    alpha, *totals = lax.optimization_barrier((alpha, *totals))
    swapped = moved(alpha, mate_of)
    totals = view(1, alpha, totals)
    totals = view(2, swapped, totals)
    return view(3, beta, totals, last=True).transpose(1, 0, 2)


def solution(mesh):
    return jax.shard_map(
        per_device,
        mesh=mesh,
        in_specs=(
            P(("groups", "scene"), None, None),
            P(),
            P(),
            P(),
            P(),
            P(),
            P(),
            P("groups", None),
            P("groups"),
        ),
        out_specs=P(("groups", "scene"), None, None),
        check_vma=False,
    )
```

time: 44 us -> 26.3 us (0.60)
  local copies, waits for them, and re-layouts: 10.6 us -> 0.01 us
  waiting for transfers between devices: 11.6 us -> 3.24 us
  starting transfers between devices: 6.11 us -> 6.67 us
    ppermute x4, waiting for transfers between devices: 11.6 us -> 3.24 us  [moved(): lax.ppermute(value, 'scene', [(s, target_of(s) % scene_size) for s in ran...]
    unnamed x23 -> x2, local copies, waits for them, and re-layouts: 7.77 us -> 0.01 us
    broadcast_in_dim x1 -> x0, local copies, waits for them, and re-layouts: 1.44 us -> none  [per_device(): return joined[None]]
    reshape x2 -> x0, local copies, waits for them, and re-layouts: 1.38 us -> none  [the longest x1 0.69 us: per_device(): head_gain.reshape(1, -1)]
    ppermute x4, starting transfers between devices: 6.11 us -> 6.67 us  [moved(): lax.ppermute(value, 'scene', [(s, target_of(s) % scene_size) for s in ran...]
    pallas_call x3 -> x5, Pallas kernels: 15.8 us -> 16.2 us  [the longest x4 13.1 us: view(): pl.pallas_call(functools.partial(view_kernel, at, not totals, last), out_...]
  transfers between devices with their start and end apart: 4 -> 4, of which waited for: 2 -> 1; matrix products, arithmetic and copies ran while one was open for 5% -> 0% of each run, Pallas kernels for 27% -> 46%
where the time goes in v2:
time: 26.3 us; the launch traced here: 26.2 us
  Pallas kernels  16.2 us (62%)
  starting transfers between devices  6.67 us (25%)
  waiting for transfers between devices  3.24 us (12%)
    pallas_call x4, Pallas kernels, view(): pl.pallas_call(functools.partial(view_kernel, at, not totals, last), out_...  13.1 us
    ppermute x4, starting transfers between devices, moved(): lax.ppermute(value, 'scene', [(s, target_of(s) % scene_size) for s in ran...  6.67 us
    ppermute x4, waiting for transfers between devices, moved(): lax.ppermute(value, 'scene', [(s, target_of(s) % scene_size) for s in ran...  3.24 us
    pallas_call x1, Pallas kernels, per_device(): pl.pallas_call(functools.partial(first_kernel, scene_size, slots, offsets...  3.1 us
  transfers between devices with their start and end apart: 4, of which 1 were waited for; matrix products, arithmetic and copies ran while one was open for 0% of the time, Pallas kernels for 46%

profile of v2, /device:TPU:0, one launch (start us, length us, event | category | flops | bytes accessed | tf_op | source)
XLA Modules:
  0.0 26.2 jit_solution(6339680635276646525)
XLA Ops:
  0.0 0.5 %collective-permute-start.2 = (bf16[196,768]{1,0:T(8,128)(2,1)}, bf16[196,768]{1,0:T(8,128)(2,1)S(1)}, u32[]{:S(2)}, u32[]{:S(2)}) collective-permute-start(bf16[196,768]{1,0:T(8,128)(2,1)} %bitcast.3), channel_id=1, source_target_pairs={{0,1},{1,0},{2,3},{3,2},{4,5},{5,4},{6,7},{7,6},{8,9},{9,8},{10,11... | collective-permute-start | bytes 903176 | tf_op jit(solution)/shard_map/ppermute | solution.py:229
  0.5 5.7 %collective-permute-start.1 = (bf16[196,768]{1,0:T(8,128)(2,1)}, bf16[196,768]{1,0:T(8,128)(2,1)S(1)}, u32[]{:S(2)}, u32[]{:S(2)}) collective-permute-start(bf16[196,768]{1,0:T(8,128)(2,1)} %bitcast.4), channel_id=1, source_target_pairs={{0,15},{1,2},{2,1},{3,4},{4,3},{5,6},{6,5},{7,8},{8,7},{9,10},{10,... | collective-permute-start | bytes 903176 | tf_op jit(solution)/shard_map/ppermute | solution.py:229
  6.1 3.1 %load_queries.1 = (bf16[196,768]{1,0:T(8,128)(2,1)S(1)}, bf16[768,1536]{1,0:T(8,128)(2,1)S(1)}, bf16[768,768]{1,0:T(8,128)(2,1)S(1)}, bf16[768,1024]{1,0:T(8,128...) custom-call(bf16[1,196,768]{2,1,0:T(8,128)(2,1)} %tokens_hbm.1, ...), custom_call_target="tpu_custom_call" | custom-call | flops 924844032 | bytes 1048576 | tf_op jit(solution)/shard_map/load_queries/pallas_call | solution.py:255
  9.3 0.0 collective-permute-done.2.partner_ref
  9.3 0.0 copy-start
  9.3 3.0 %shard_map.91 = (f32[196,768]{1,0:T(8,128)S(1)}, f32[196,256]{1,0:T(8,128)S(1)}) custom-call(bf16[196,768]{1,0:T(8,128)(2,1)S(1)} %get-tuple-element.24.own_ref, bf16[768,1536]{1,0:T(8,128)(2,1)S(1)} %get-tuple-element.25.kv_ref, bf16[768,768]{1,0:T(8,128)(2,1)S(1)} %get-tuple-element.26.out_ref, bf16[768,1024]{1,0:T(8,128)(2,1)S(1)} %get-tuple-element.27.head_ref, ...), custom_call_target="tpu_custom_call" | custom-call | flops 924844032 | bytes 1048576 | tf_op jit(solution)/shard_map/pallas_call | solution.py:282
  12.2 0.0 collective-permute-done.1.partner_ref
  12.3 0.1 collective-permute-start.3
  12.3 0.0 copy-done
  12.3 0.4 %collective-permute-start = (bf16[196,768]{1,0:T(8,128)(2,1)S(1)}, bf16[196,768]{1,0:T(8,128)(2,1)S(1)}, u32[]{:S(2)}, u32[]{:S(2)}) collective-permute-start(bf16[196,768]{1,0:T(8,128)(2,1)S(1)} %bitcast.5), channel_id=1, source_target_pairs={{0,2},{1,15},{2,4},{3,1},{4,6},{5,3},{6,8},{7,5},{8,10},{9,7},{10,... | collective-permute-start | bytes 903176 | tf_op jit(solution)/shard_map/ppermute | solution.py:229
  12.8 3.0 %shard_map.92 = (f32[196,768]{1,0:T(8,128)S(1)}, f32[196,256]{1,0:T(8,128)S(1)}) custom-call(bf16[196,768]{1,0:T(8,128)(2,1)S(1)} %get-tuple-element.24.own_ref, bf16[768,1536]{1,0:T(8,128)(2,1)S(1)} %get-tuple-element.25.kv_ref, bf16[768,768]{1,0:T(8,128)(2,1)S(1)} %get-tuple-element.26.out_ref, bf16[768,1024]{1,0:T(8,128)(2,1)S(1)} %get-tuple-element.27.head_ref, ...), custom_call_target="tpu_custom_call" | custom-call | flops 924844032 | bytes 1048576 | tf_op jit(solution)/shard_map/pallas_call | solution.py:282
  15.8 0.0 collective-permute-done.3.partner_ref
  15.8 3.0 %shard_map.93 = (f32[196,768]{1,0:T(8,128)S(1)}, f32[196,256]{1,0:T(8,128)S(1)}) custom-call(bf16[196,768]{1,0:T(8,128)(2,1)S(1)} %get-tuple-element.24.own_ref, bf16[768,1536]{1,0:T(8,128)(2,1)S(1)} %get-tuple-element.25.kv_ref, bf16[768,768]{1,0:T(8,128)(2,1)S(1)} %get-tuple-element.26.out_ref, bf16[768,1024]{1,0:T(8,128)(2,1)S(1)} %get-tuple-element.27.head_ref, ...), custom_call_target="tpu_custom_call" | custom-call | flops 924844032 | bytes 1048576 | tf_op jit(solution)/shard_map/pallas_call | solution.py:282
  18.8 3.2 %collective-permute-done.partner_ref = bf16[196,768]{1,0:T(8,128)(2,1)S(1)} collective-permute-done((bf16[196,768]{1,0:T(8,128)(2,1)S(1)}, bf16[196,768]{1,0:T(8,128)(2,1)S(1)}, u32[]{:S(2)}, u32[]{:S(2)}) %collective-permute-start) | collective-permute-done | bytes 301088 | tf_op jit(solution)/shard_map/ppermute | solution.py:229
  22.0 4.2 %shard_map.94 = f32[196,1,768]{2,1,0:T(1,128)} custom-call(bf16[196,768]{1,0:T(8,128)(2,1)S(1)} %get-tuple-element.24.own_ref, bf16[768,1536]{1,0:T(8,128)(2,1)S(1)} %get-tuple-element.25.kv_ref, bf16[768,768]{1,0:T(8,128)(2,1)S(1)} %get-tuple-element.26.out_ref, bf16[768,1024]{1,0:T(8,128)(2,1)S(1)} %get-tuple-element.27.head_ref, ...), custom_call_target="tpu_custom_call" | custom-call | flops 924844032 | bytes 1048576 | tf_op jit(solution)/shard_map/pallas_call | solution.py:282
Async XLA Ops:
  0.0 9.3 %collective-permute-start.2 = (bf16[196,768]{1,0:T(8,128)(2,1)}, bf16[196,768]{1,0:T(8,128)(2,1)S(1)}, u32[]{:S(2)}, u32[]{:S(2)}) collective-permute-start(bf16[196,768]{1,0:T(8,128)(2,1)} %bitcast.3), channel_id=1, source_target_pairs={{0,1},{1,0},{2,3},{3,2},{4,5},{5,4},{6,7},{7,6},{8,9},{9,8},{10,11... | collective-permute-start | bytes 903176 | tf_op jit(solution)/shard_map/ppermute | solution.py:229
  0.5 11.7 %collective-permute-start.1 = (bf16[196,768]{1,0:T(8,128)(2,1)}, bf16[196,768]{1,0:T(8,128)(2,1)S(1)}, u32[]{:S(2)}, u32[]{:S(2)}) collective-permute-start(bf16[196,768]{1,0:T(8,128)(2,1)} %bitcast.4), channel_id=1, source_target_pairs={{0,15},{1,2},{2,1},{3,4},{4,3},{5,6},{6,5},{7,8},{8,7},{9,10},{10,... | collective-permute-start | bytes 903176 | tf_op jit(solution)/shard_map/ppermute | solution.py:229
  9.3 3.1 %copy-start = (bf16[1,196,768]{2,1,0:T(8,128)(2,1)S(1)}, bf16[1,196,768]{2,1,0:T(8,128)(2,1)}, u32[]{:S(2)}) copy-start(bf16[1,196,768]{2,1,0:T(8,128)(2,1)} %tokens_hbm.1) | copy-start | bytes 903172
  12.3 3.5 %collective-permute-start.3 = (bf16[196,768]{1,0:T(8,128)(2,1)S(1)}, bf16[196,768]{1,0:T(8,128)(2,1)S(1)}, u32[]{:S(2)}, u32[]{:S(2)}) collective-permute-start(bf16[196,768]{1,0:T(8,128)(2,1)S(1)} %collective-permute-done.1.partner_ref), channel_id=1, source_target_pairs={{0,1},{1,0},{2,3},{3,2},{4,5},{5,4},{6,7},{7,6},{8,9},{9,8},{10,11... | collective-permute-start | bytes 903176 | tf_op jit(solution)/shard_map/ppermute | solution.py:229
  12.3 9.7 %collective-permute-start = (bf16[196,768]{1,0:T(8,128)(2,1)S(1)}, bf16[196,768]{1,0:T(8,128)(2,1)S(1)}, u32[]{:S(2)}, u32[]{:S(2)}) collective-permute-start(bf16[196,768]{1,0:T(8,128)(2,1)S(1)} %bitcast.5), channel_id=1, source_target_pairs={{0,2},{1,15},{2,4},{3,1},{4,6},{5,3},{6,8},{7,5},{8,10},{9,7},{10,... | collective-permute-start | bytes 903176 | tf_op jit(solution)/shard_map/ppermute | solution.py:229

commit v3 on v2

--- a/solution.py
+++ b/solution.py
@@ -58,7 +58,7 @@
     return count
 
 
-def one_view(partner, count_row, own_ref, q_ref, kv_ref, out_ref, head_ref, gains_ref, bias_ref, keys_scr, vals_scr, att_scr, emit):
+def one_view(partner, count_row, own_ref, q_ref, qkv_ref, out_ref, head_ref, gains_ref, bias_ref, keys_scr, vals_scr, att_scr, loads, emit):
     tokens, width = own_ref.shape
     head_size = width // HEADS
     pixels = head_ref.shape[1] // 4
@@ -78,8 +78,8 @@
 
     normed = layer_norm(partner.astype(jnp.float32), gains_ref[0:1, :]).astype(jnp.bfloat16)
     for start in range(0, width, MXU):
-        keys_scr[:tokens, start : start + MXU] = head_unit(matmul(normed, kv_ref[:, start : start + MXU]), block)
-        value = matmul(normed, kv_ref[:, width + start : width + start + MXU]).astype(jnp.bfloat16)
+        keys_scr[:tokens, start : start + MXU] = head_unit(matmul(normed, qkv_ref[:, width + start : width + start + MXU]), block)
+        value = matmul(normed, qkv_ref[:, 2 * width + start : 2 * width + start + MXU]).astype(jnp.bfloat16)
         for half in range(MXU // LANES):
             vals_scr[start // LANES + half, :tokens, :LANES] = value[:, half * LANES : (half + 1) * LANES]
     for pair in range(pairs):
@@ -94,6 +94,8 @@
         top = jnp.where(low_head, mixed[:tokens, :LANES], mixed[rows : rows + tokens, :LANES])
         norm = jnp.where(low_head, mixed[:tokens, LANES:], mixed[rows : rows + tokens, LANES:])
         att_scr[:, pair * LANES : (pair + 1) * LANES] = (top / norm).astype(jnp.bfloat16)
+    for load in loads:
+        load.wait()
     mixed = own_ref[...].astype(jnp.float32) + matmul(att_scr[...], out_ref[...])
     head_in = layer_norm(mixed, gains_ref[1:2, :]).astype(jnp.bfloat16)
     conf = matmul(head_in, head_ref[:, 3 * pixels :]) + bias_ref[:, 3 * pixels :]
@@ -120,17 +122,12 @@
     offsets_of,
     tokens_hbm,
     qkv_hbm,
-    out_hbm,
     attn_gain_hbm,
     head_gain_hbm,
-    head_hbm,
     bias_hbm,
     list_hbm,
     count_hbm,
     own_ref,
-    kv_ref,
-    out_ref,
-    head_ref,
     gains_ref,
     bias_ref,
     counts_ref,
@@ -151,10 +148,6 @@
         (bias_hbm, bias_ref.at[0]),
         (list_hbm, list_smem),
         (count_hbm, count_smem),
-        (qkv_hbm.at[:, width : 2 * width], kv_ref.at[:, :width]),
-        (qkv_hbm.at[:, 2 * width :], kv_ref.at[:, width:]),
-        (out_hbm, out_ref),
-        (head_hbm, head_ref),
     ]
     copies = [pltpu.make_async_copy(source, target, sems.at[at]) for at, (source, target) in enumerate(plan)]
     for copy in copies:
@@ -183,14 +176,22 @@
 
 
 def view_kernel(
-    at, first, last, own_ref, kv_ref, out_ref, head_ref, gains_ref, bias_ref, counts_ref, q_ref, partner_ref, *refs
+    at, first, last, own_ref, gains_ref, bias_ref, counts_ref, q_ref, qkv_ref, out_ref, head_ref, partner_ref, *refs
 ):
-    if not first:
-        sums_in, weights_in, *refs = refs
-    if last:
-        joined_hbm, keys_scr, vals_scr, att_scr, joined_scr, sems = refs
+    loads = ()
+    if first:
+        sums_ref, weights_ref, out_vmem, head_vmem, keys_scr, vals_scr, att_scr, load_sems = refs
+        loads = (
+            pltpu.make_async_copy(out_ref, out_vmem, load_sems.at[0]),
+            pltpu.make_async_copy(head_ref, head_vmem, load_sems.at[1]),
+        )
+        for load in loads:
+            load.start()
+        out_ref, head_ref = out_vmem, head_vmem
+    elif last:
+        sums_in, weights_in, joined_hbm, keys_scr, vals_scr, att_scr, joined_scr, sems = refs
     else:
-        sums_ref, weights_ref, keys_scr, vals_scr, att_scr = refs
+        sums_in, weights_in, sums_ref, weights_ref, keys_scr, vals_scr, att_scr = refs
     copies = []
 
     def emit(part, cols, weight, weighted):
@@ -207,11 +208,15 @@
                 weights_ref[...] = weight
 
     one_view(
-        partner_ref[...], counts_ref[at, 0:1, 0:1], own_ref, q_ref, kv_ref, out_ref, head_ref, gains_ref, bias_ref,
-        keys_scr, vals_scr, att_scr, emit,
+        partner_ref[...], counts_ref[at, 0:1, 0:1], own_ref, q_ref, qkv_ref, out_ref, head_ref, gains_ref, bias_ref,
+        keys_scr, vals_scr, att_scr, loads, emit,
     )
     for copy in copies:
         copy.wait()
+
+
+def anchor_kernel(counts_in, weights_ref, counts_ref):
+    counts_ref[...] = counts_in[...]
 
 
 def per_device(
@@ -244,9 +249,6 @@
     mate = moved(own, mate_of)
     first_shapes = (
         jax.ShapeDtypeStruct((token_count, width), bf16),
-        jax.ShapeDtypeStruct((width, 2 * width), bf16),
-        jax.ShapeDtypeStruct(out_weight.shape, bf16),
-        jax.ShapeDtypeStruct(head_weight.shape, bf16),
         jax.ShapeDtypeStruct((2, width), f32),
         jax.ShapeDtypeStruct((1, columns), f32),
         jax.ShapeDtypeStruct((4, 8, LANES), f32),
@@ -255,49 +257,65 @@
     state = pl.pallas_call(
         functools.partial(first_kernel, scene_size, slots, offsets_of),
         out_shape=first_shapes,
-        in_specs=[HBM_SPEC] * 9,
+        in_specs=[HBM_SPEC] * 7,
         out_specs=tuple(VMEM_SPEC for _ in first_shapes),
         scratch_shapes=[
             pltpu.VMEM((width, width), bf16),
             pltpu.SMEM((2, pair_list.shape[0]), jnp.int32),
             pltpu.SMEM(pair_count.shape, jnp.int32),
-            pltpu.SemaphoreType.DMA((11,)),
+            pltpu.SemaphoreType.DMA((7,)),
         ],
         compiler_params=params,
-        cost_estimate=cost,
+        cost_estimate=pl.CostEstimate(flops=cost.flops, bytes_accessed=64 * 2**20, transcendentals=0),
         name="load_queries",
     )(
         in_hbm(tokens),
-        *(in_hbm(value) for value in (qkv_weight, out_weight, attn_gain, head_gain, head_weight, head_bias)),
+        *(in_hbm(value) for value in (qkv_weight, attn_gain, head_gain, head_bias)),
         in_hbm(pair_list.T),
         in_hbm(pair_count),
     )
 
-    def view(at, partner, totals, last=False):
-        out_shape = jax.ShapeDtypeStruct((token_count, 1, 3 * pixels), f32) if last else (sums, weights)
+    def view(at, partner, weights_now, totals, last=False):
+        first = not totals
+        operands = [*state, qkv_weight, *weights_now, partner, *totals]
+        in_specs = [VMEM_SPEC] * len(operands)
         scratch = view_scratch(token_count, width)
+        out_shape = [sums, weights]
+        if first:
+            out_shape += [jax.ShapeDtypeStruct(value.shape, value.dtype) for value in weights_now]
+            in_specs[6:8] = [HBM_SPEC] * 2
+            scratch += [pltpu.SemaphoreType.DMA((2,))]
         if last:
+            out_shape = [jax.ShapeDtypeStruct((token_count, 1, 3 * pixels), f32)]
             scratch += [pltpu.VMEM(sums.shape, f32), pltpu.SemaphoreType.DMA((3,))]
-        operands = (*state, partner, *totals)
         return pl.pallas_call(
-            functools.partial(view_kernel, at, not totals, last),
+            functools.partial(view_kernel, at, first, last),
             out_shape=out_shape,
-            in_specs=[VMEM_SPEC] * len(operands),
-            out_specs=HBM_SPEC if last else (VMEM_SPEC, VMEM_SPEC),
+            in_specs=in_specs,
+            out_specs=[HBM_SPEC if last else VMEM_SPEC] * len(out_shape),
             scratch_shapes=scratch,
             compiler_params=params,
             cost_estimate=cost,
         )(*operands)
 
-    own, queries = lax.optimization_barrier((own, state[-1]))
-    state = (*state[:-1], queries)
+    *totals, out_vmem, head_vmem = view(0, mate, (in_hbm(out_weight), in_hbm(head_weight)), ())
+    weights_now = (out_vmem, head_vmem)
+    own, *totals = lax.optimization_barrier((own, *totals))
     beta = moved(own, lambda s: s - 2 if s % 2 else s + 2)
-    totals = view(0, mate, ())
+    counts = pl.pallas_call(
+        anchor_kernel,
+        out_shape=first_shapes[3],
+        in_specs=[VMEM_SPEC] * 2,
+        out_specs=VMEM_SPEC,
+        compiler_params=params,
+        name="anchor",
+    )(state[3], totals[1])
+    state = (*state[:3], counts, state[4])
     alpha, *totals = lax.optimization_barrier((alpha, *totals))
     swapped = moved(alpha, mate_of)
-    totals = view(1, alpha, totals)
-    totals = view(2, swapped, totals)
-    return view(3, beta, totals, last=True).transpose(1, 0, 2)
+    totals = view(1, alpha, weights_now, totals)
+    totals = view(2, swapped, weights_now, totals)
+    return view(3, beta, weights_now, totals, last=True)[0].transpose(1, 0, 2)
 
 
 def solution(mesh):

time: 26.3 us -> 26.3 us (level)
    pallas_call x4 -> x5, Pallas kernels: 13.1 us -> 13.2 us  [the longest x4 13.2 us: view(): pl.pallas_call(functools.partial(view_kernel, at, first, last), out_shape...]
where the time goes in v3:
time: 26.3 us; the launch traced here: 26.2 us
  Pallas kernels  16.1 us (61%)
  starting transfers between devices  6.68 us (25%)
  waiting for transfers between devices  3.24 us (12%)
    pallas_call x4, Pallas kernels, view(): pl.pallas_call(functools.partial(view_kernel, at, first, last), out_shape...  13.2 us
    ppermute x4, starting transfers between devices, moved(): lax.ppermute(value, 'scene', [(s, target_of(s) % scene_size) for s in ran...  6.68 us
    ppermute x4, waiting for transfers between devices, moved(): lax.ppermute(value, 'scene', [(s, target_of(s) % scene_size) for s in ran...  3.24 us
    pallas_call x1, Pallas kernels, per_device(): pl.pallas_call(functools.partial(first_kernel, scene_size, slots, offsets...  2.9 us
  transfers between devices with their start and end apart: 4, of which 1 were waited for; matrix products, arithmetic and copies ran while one was open for 0% of the time, Pallas kernels for 46%

profile of v3, /device:TPU:0, one launch (start us, length us, event | category | flops | bytes accessed | tf_op | source)
XLA Modules:
  0.0 26.2 jit_solution(11328728222598075388)
XLA Ops:
  0.0 0.5 %collective-permute-start = (bf16[196,768]{1,0:T(8,128)(2,1)}, bf16[196,768]{1,0:T(8,128)(2,1)S(1)}, u32[]{:S(2)}, u32[]{:S(2)}) collective-permute-start(bf16[196,768]{1,0:T(8,128)(2,1)} %bitcast.3), channel_id=1, source_target_pairs={{0,1},{1,0},{2,3},{3,2},{4,5},{5,4},{6,7},{7,6},{8,9},{9,8},{10,11... | collective-permute-start | bytes 903176 | tf_op jit(solution)/shard_map/ppermute | solution.py:234
  0.5 5.7 %collective-permute-start.2 = (bf16[196,768]{1,0:T(8,128)(2,1)}, bf16[196,768]{1,0:T(8,128)(2,1)S(1)}, u32[]{:S(2)}, u32[]{:S(2)}) collective-permute-start(bf16[196,768]{1,0:T(8,128)(2,1)} %bitcast.4), channel_id=1, source_target_pairs={{0,15},{1,2},{2,1},{3,4},{4,3},{5,6},{6,5},{7,8},{8,7},{9,10},{10,... | collective-permute-start | bytes 903176 | tf_op jit(solution)/shard_map/ppermute | solution.py:234
  6.1 0.0 copy-start
  6.2 2.9 %load_queries.1 = (bf16[196,768]{1,0:T(8,128)(2,1)S(1)}, f32[2,768]{1,0:T(2,128)S(1)}, f32[1,1024]{1,0:T(1,128)S(1)}, f32[4,8,128]{2,1,0:T(8,128)S(1)}, bf16[6,416,128]{2,1,0:T(8,128)(2,1)S(1)}) custom-call(bf16[1,196,768]{2,1,0:T(8,128)(2,1)} %tokens_hbm.1, bf16[768,2304]{1,0:T(8,128)(2,1)} %qkv_ref.7, f32[768]{0:T(1024)} %attn_gain_hbm.1, ...), custom_call_target="tpu_custom_call" | custom-call | flops 924844032 | bytes 67108864 | tf_op jit(solution)/shard_map/load_queries/pallas_call | solution.py:257
  9.1 0.0 collective-permute-done.partner_ref
  9.1 0.0 copy-done
  9.1 0.0 copy-start.1
  9.1 3.1 %shard_map.91 = (f32[196,768]{1,0:T(8,128)S(1)}, f32[196,256]{1,0:T(8,128)S(1)}, bf16[768,768]{1,0:T(8,128)(2,1)S(1)}, bf16[768,1024]{1,0:T(8,128)(2,1)S(1)}) custom-call(bf16[196,768]{1,0:T(8,128)(2,1)S(1)} %get-tuple-element.24.own_ref, f32[2,768]{1,0:T(2,128)S(1)} %get-tuple-element.25.gains_ref, f32[1,1024]{1,0:T(1,128)S(1)} %get-tuple-element.26.bias_ref, ...), custom_call_target="tpu_custom_call" | custom-call | flops 924844032 | bytes 1048576 | tf_op jit(solution)/shard_map/pallas_call | solution.py:291
  12.2 0.0 collective-permute-done.2.partner_ref
  12.2 0.1 collective-permute-start.3
  12.3 0.0 copy-done.1
  12.3 0.5 %collective-permute-start.1 = (bf16[196,768]{1,0:T(8,128)(2,1)S(1)}, bf16[196,768]{1,0:T(8,128)(2,1)S(1)}, u32[]{:S(2)}, u32[]{:S(2)}) collective-permute-start(bf16[196,768]{1,0:T(8,128)(2,1)S(1)} %bitcast.5), channel_id=1, source_target_pairs={{0,2},{1,15},{2,4},{3,1},{4,6},{5,3},{6,8},{7,5},{8,10},{9,7},{10,... | collective-permute-start | bytes 903176 | tf_op jit(solution)/shard_map/ppermute | solution.py:234
  12.8 3.0 %shard_map.92 = (f32[196,768]{1,0:T(8,128)S(1)}, f32[196,256]{1,0:T(8,128)S(1)}) custom-call(bf16[196,768]{1,0:T(8,128)(2,1)S(1)} %get-tuple-element.24.own_ref, f32[2,768]{1,0:T(2,128)S(1)} %get-tuple-element.25.gains_ref, f32[1,1024]{1,0:T(1,128)S(1)} %get-tuple-element.26.bias_ref, f32[4,8,128]{2,1,0:T(8,128)S(1)} %anchor.1.counts_ref, ...), custom_call_target="tpu_custom_call" | custom-call | flops 924844032 | bytes 1048576 | tf_op jit(solution)/shard_map/pallas_call | solution.py:291
  15.8 0.0 collective-permute-done.3.partner_ref
  15.8 3.0 %shard_map.93 = (f32[196,768]{1,0:T(8,128)S(1)}, f32[196,256]{1,0:T(8,128)S(1)}) custom-call(bf16[196,768]{1,0:T(8,128)(2,1)S(1)} %get-tuple-element.24.own_ref, f32[2,768]{1,0:T(2,128)S(1)} %get-tuple-element.25.gains_ref, f32[1,1024]{1,0:T(1,128)S(1)} %get-tuple-element.26.bias_ref, f32[4,8,128]{2,1,0:T(8,128)S(1)} %anchor.1.counts_ref, ...), custom_call_target="tpu_custom_call" | custom-call | flops 924844032 | bytes 1048576 | tf_op jit(solution)/shard_map/pallas_call | solution.py:291
  18.8 3.2 %collective-permute-done.1.partner_ref = bf16[196,768]{1,0:T(8,128)(2,1)S(1)} collective-permute-done((bf16[196,768]{1,0:T(8,128)(2,1)S(1)}, bf16[196,768]{1,0:T(8,128)(2,1)S(1)}, u32[]{:S(2)}, u32[]{:S(2)}) %collective-permute-start.1) | collective-permute-done | bytes 301088 | tf_op jit(solution)/shard_map/ppermute | solution.py:234
  22.0 4.2 %shard_map.94 = f32[196,1,768]{2,1,0:T(1,128)} custom-call(bf16[196,768]{1,0:T(8,128)(2,1)S(1)} %get-tuple-element.24.own_ref, f32[2,768]{1,0:T(2,128)S(1)} %get-tuple-element.25.gains_ref, f32[1,1024]{1,0:T(1,128)S(1)} %get-tuple-element.26.bias_ref, f32[4,8,128]{2,1,0:T(8,128)S(1)} %anchor.1.counts_ref, bf16[6,416,128]{2,1,0:T(8,128)(2,1)S(1)} %get-tuple-element.28.q_ref, ...), custom_call_target="tpu_custom_call" | custom-call | flops 924844032 | bytes 1048576 | tf_op jit(solution)/shard_map/pallas_call | solution.py:291
  (1 shorter events, 0.0 us)
Async XLA Ops:
  0.0 9.1 %collective-permute-start = (bf16[196,768]{1,0:T(8,128)(2,1)}, bf16[196,768]{1,0:T(8,128)(2,1)S(1)}, u32[]{:S(2)}, u32[]{:S(2)}) collective-permute-start(bf16[196,768]{1,0:T(8,128)(2,1)} %bitcast.3), channel_id=1, source_target_pairs={{0,1},{1,0},{2,3},{3,2},{4,5},{5,4},{6,7},{7,6},{8,9},{9,8},{10,11... | collective-permute-start | bytes 903176 | tf_op jit(solution)/shard_map/ppermute | solution.py:234
  0.5 11.7 %collective-permute-start.2 = (bf16[196,768]{1,0:T(8,128)(2,1)}, bf16[196,768]{1,0:T(8,128)(2,1)S(1)}, u32[]{:S(2)}, u32[]{:S(2)}) collective-permute-start(bf16[196,768]{1,0:T(8,128)(2,1)} %bitcast.4), channel_id=1, source_target_pairs={{0,15},{1,2},{2,1},{3,4},{4,3},{5,6},{6,5},{7,8},{8,7},{9,10},{10,... | collective-permute-start | bytes 903176 | tf_op jit(solution)/shard_map/ppermute | solution.py:234
  6.1 2.9 %copy-start = (bf16[768,2304]{1,0:T(8,128)(2,1)S(1)}, bf16[768,2304]{1,0:T(8,128)(2,1)}, u32[]{:S(2)}) copy-start(bf16[768,2304]{1,0:T(8,128)(2,1)} %qkv_ref.7) | copy-start | bytes 10616836
  9.1 3.2 %copy-start.1 = (bf16[1,196,768]{2,1,0:T(8,128)(2,1)S(1)}, bf16[1,196,768]{2,1,0:T(8,128)(2,1)}, u32[]{:S(2)}) copy-start(bf16[1,196,768]{2,1,0:T(8,128)(2,1)} %tokens_hbm.1) | copy-start | bytes 903172
  12.2 3.5 %collective-permute-start.3 = (bf16[196,768]{1,0:T(8,128)(2,1)S(1)}, bf16[196,768]{1,0:T(8,128)(2,1)S(1)}, u32[]{:S(2)}, u32[]{:S(2)}) collective-permute-start(bf16[196,768]{1,0:T(8,128)(2,1)S(1)} %collective-permute-done.2.partner_ref), channel_id=1, source_target_pairs={{0,1},{1,0},{2,3},{3,2},{4,5},{5,4},{6,7},{7,6},{8,9},{9,8},{10,11... | collective-permute-start | bytes 903176 | tf_op jit(solution)/shard_map/ppermute | solution.py:234
  12.3 9.7 %collective-permute-start.1 = (bf16[196,768]{1,0:T(8,128)(2,1)S(1)}, bf16[196,768]{1,0:T(8,128)(2,1)S(1)}, u32[]{:S(2)}, u32[]{:S(2)}) collective-permute-start(bf16[196,768]{1,0:T(8,128)(2,1)S(1)} %bitcast.5), channel_id=1, source_target_pairs={{0,2},{1,15},{2,4},{3,1},{4,6},{5,3},{6,8},{7,5},{8,10},{9,7},{10,... | collective-permute-start | bytes 903176 | tf_op jit(solution)/shard_map/ppermute | solution.py:234

commit v4 on v3

--- a/solution.py
+++ b/solution.py
@@ -58,7 +58,7 @@
     return count
 
 
-def one_view(partner, count_row, own_ref, q_ref, qkv_ref, out_ref, head_ref, gains_ref, bias_ref, keys_scr, vals_scr, att_scr, loads, emit):
+def one_view(normed, count_row, own_ref, q_ref, kv_ref, out_ref, head_ref, gains_ref, bias_ref, keys_scr, vals_scr, att_scr, loads, emit):
     tokens, width = own_ref.shape
     head_size = width // HEADS
     pixels = head_ref.shape[1] // 4
@@ -76,10 +76,9 @@
         vals_scr[pair, tail:, :LANES] = jnp.zeros((padded - tail, LANES), jnp.bfloat16)
         vals_scr[pair, :, LANES:] = ones
 
-    normed = layer_norm(partner.astype(jnp.float32), gains_ref[0:1, :]).astype(jnp.bfloat16)
     for start in range(0, width, MXU):
-        keys_scr[:tokens, start : start + MXU] = head_unit(matmul(normed, qkv_ref[:, width + start : width + start + MXU]), block)
-        value = matmul(normed, qkv_ref[:, 2 * width + start : 2 * width + start + MXU]).astype(jnp.bfloat16)
+        keys_scr[:tokens, start : start + MXU] = head_unit(matmul(normed, kv_ref[:, start : start + MXU]), block)
+        value = matmul(normed, kv_ref[:, width + start : width + start + MXU]).astype(jnp.bfloat16)
         for half in range(MXU // LANES):
             vals_scr[start // LANES + half, :tokens, :LANES] = value[:, half * LANES : (half + 1) * LANES]
     for pair in range(pairs):
@@ -128,6 +127,8 @@
     list_hbm,
     count_hbm,
     own_ref,
+    normed_ref,
+    kv_ref,
     gains_ref,
     bias_ref,
     counts_ref,
@@ -140,33 +141,40 @@
     tokens, width = own_ref.shape
     head_size = width // HEADS
     rows = q_ref.shape[1] // 2
+    first_cols = [slice(start, start + MXU) for start in range(0, width, MXU)]
     plan = [
         (tokens_hbm.at[0], own_ref),
         (attn_gain_hbm, gains_ref.at[0]),
-        (qkv_hbm.at[:, :width], wq_scr),
+        *((qkv_hbm.at[:, cols], wq_scr.at[:, cols]) for cols in first_cols),
+        (list_hbm, list_smem),
+        (count_hbm, count_smem),
         (head_gain_hbm, gains_ref.at[1]),
         (bias_hbm, bias_ref.at[0]),
-        (list_hbm, list_smem),
-        (count_hbm, count_smem),
+        (qkv_hbm.at[:, width : 2 * width], kv_ref.at[:, :width]),
+        (qkv_hbm.at[:, 2 * width :], kv_ref.at[:, width:]),
     ]
     copies = [pltpu.make_async_copy(source, target, sems.at[at]) for at, (source, target) in enumerate(plan)]
     for copy in copies:
         copy.start()
-    for copy in copies[:3]:
-        copy.wait()
     low_head = lax.broadcasted_iota(jnp.int32, (1, LANES), 1) < head_size
     block = head_block(head_size)
-    normed = layer_norm(own_ref[...].astype(jnp.float32), gains_ref[0:1, :]).astype(jnp.bfloat16)
-    q_ref[...] = jnp.zeros_like(q_ref)
-    for start in range(0, width, MXU):
-        unit = head_unit(matmul(normed, wq_scr[:, start : start + MXU]), block)
+    tail = tokens // 16 * 16
+    for half in range(2):
+        q_ref[:, half * rows + tail : (half + 1) * rows, :] = jnp.zeros((q_ref.shape[0], rows - tail, LANES), jnp.bfloat16)
+    for copy in copies[:2]:
+        copy.wait()
+    normed_ref[...] = layer_norm(own_ref[...].astype(jnp.float32), gains_ref[0:1, :]).astype(jnp.bfloat16)
+    normed = normed_ref[...]
+    for at, cols in enumerate(first_cols):
+        copies[2 + at].wait()
+        unit = head_unit(matmul(normed, wq_scr[:, cols]), block)
         for half in range(MXU // LANES):
-            pair = start // LANES + half
+            pair = cols.start // LANES + half
             piece = unit[:, half * LANES : (half + 1) * LANES]
             zero = jnp.zeros_like(piece)
             q_ref[pair, :tokens, :] = jnp.where(low_head, piece, zero)
             q_ref[pair, rows : rows + tokens, :] = jnp.where(low_head, zero, piece)
-    for copy in copies[3:]:
+    for copy in copies[2 + len(first_cols) :]:
         copy.wait()
     position = lax.axis_index("scene")
     for at, offset in enumerate(offsets_of(position)):
@@ -176,7 +184,7 @@
 
 
 def view_kernel(
-    at, first, last, own_ref, gains_ref, bias_ref, counts_ref, q_ref, qkv_ref, out_ref, head_ref, partner_ref, *refs
+    at, first, last, own_ref, gains_ref, bias_ref, counts_ref, q_ref, kv_ref, out_ref, head_ref, partner_ref, *refs
 ):
     loads = ()
     if first:
@@ -198,17 +206,25 @@
         total = weighted if first else sums_in[:, cols] + weighted
         weight = weight if first else weights_in[...] + weight
         if last:
-            joined_scr[:, cols] = total / weight
-            copy = pltpu.make_async_copy(joined_scr.at[:, cols], joined_hbm.at[:, 0, cols], sems.at[part])
-            copy.start()
-            copies.append(copy)
+            ratio = total / weight
+            lines = 3 * total.shape[1] // LANES
+            for line in range(total.shape[1] // LANES):
+                rows = pl.ds(cols.start // LANES + line, total.shape[0], stride=lines)
+                joined_scr[rows, :] = ratio[:, line * LANES : (line + 1) * LANES]
+            if part == 2:
+                copy = pltpu.make_async_copy(joined_scr, joined_hbm, sems.at[0])
+                copy.start()
+                copies.append(copy)
         else:
             sums_ref[:, cols] = total
             if part == 0:
                 weights_ref[...] = weight
 
+    normed = partner_ref[...]
+    if not last:
+        normed = layer_norm(normed.astype(jnp.float32), gains_ref[0:1, :]).astype(jnp.bfloat16)
     one_view(
-        partner_ref[...], counts_ref[at, 0:1, 0:1], own_ref, q_ref, qkv_ref, out_ref, head_ref, gains_ref, bias_ref,
+        normed, counts_ref[at, 0:1, 0:1], own_ref, q_ref, kv_ref, out_ref, head_ref, gains_ref, bias_ref,
         keys_scr, vals_scr, att_scr, loads, emit,
     )
     for copy in copies:
@@ -249,12 +265,14 @@
     mate = moved(own, mate_of)
     first_shapes = (
         jax.ShapeDtypeStruct((token_count, width), bf16),
+        jax.ShapeDtypeStruct((token_count, width), bf16),
+        jax.ShapeDtypeStruct((width, 2 * width), bf16),
         jax.ShapeDtypeStruct((2, width), f32),
         jax.ShapeDtypeStruct((1, columns), f32),
         jax.ShapeDtypeStruct((4, 8, LANES), f32),
         jax.ShapeDtypeStruct((width // LANES, 2 * round_up(token_count, 16), LANES), bf16),
     )
-    state = pl.pallas_call(
+    own_vmem, normed, kv_vmem, gains, bias, counts, queries = pl.pallas_call(
         functools.partial(first_kernel, scene_size, slots, offsets_of),
         out_shape=first_shapes,
         in_specs=[HBM_SPEC] * 7,
@@ -263,10 +281,10 @@
             pltpu.VMEM((width, width), bf16),
             pltpu.SMEM((2, pair_list.shape[0]), jnp.int32),
             pltpu.SMEM(pair_count.shape, jnp.int32),
-            pltpu.SemaphoreType.DMA((7,)),
+            pltpu.SemaphoreType.DMA((8 + width // MXU,)),
         ],
         compiler_params=params,
-        cost_estimate=pl.CostEstimate(flops=cost.flops, bytes_accessed=64 * 2**20, transcendentals=0),
+        cost_estimate=cost,
         name="load_queries",
     )(
         in_hbm(tokens),
@@ -275,9 +293,9 @@
         in_hbm(pair_count),
     )
 
-    def view(at, partner, weights_now, totals, last=False):
+    def view(at, partner, counts_now, weights_now, totals, last=False):
         first = not totals
-        operands = [*state, qkv_weight, *weights_now, partner, *totals]
+        operands = [own_vmem, gains, bias, counts_now, queries, kv_vmem, *weights_now, partner, *totals]
         in_specs = [VMEM_SPEC] * len(operands)
         scratch = view_scratch(token_count, width)
         out_shape = [sums, weights]
@@ -286,8 +304,8 @@
             in_specs[6:8] = [HBM_SPEC] * 2
             scratch += [pltpu.SemaphoreType.DMA((2,))]
         if last:
-            out_shape = [jax.ShapeDtypeStruct((token_count, 1, 3 * pixels), f32)]
-            scratch += [pltpu.VMEM(sums.shape, f32), pltpu.SemaphoreType.DMA((3,))]
+            out_shape = [jax.ShapeDtypeStruct((token_count * 3 * pixels // LANES, LANES), f32)]
+            scratch += [pltpu.VMEM(out_shape[0].shape, f32), pltpu.SemaphoreType.DMA((1,))]
         return pl.pallas_call(
             functools.partial(view_kernel, at, first, last),
             out_shape=out_shape,
@@ -298,24 +316,23 @@
             cost_estimate=cost,
         )(*operands)
 
-    *totals, out_vmem, head_vmem = view(0, mate, (in_hbm(out_weight), in_hbm(head_weight)), ())
+    *totals, out_vmem, head_vmem = view(0, mate, counts, (in_hbm(out_weight), in_hbm(head_weight)), ())
     weights_now = (out_vmem, head_vmem)
-    own, *totals = lax.optimization_barrier((own, *totals))
-    beta = moved(own, lambda s: s - 2 if s % 2 else s + 2)
-    counts = pl.pallas_call(
+    normed, *totals = lax.optimization_barrier((normed, *totals))
+    beta = moved(normed, lambda s: s - 2 if s % 2 else s + 2)
+    counts_now = pl.pallas_call(
         anchor_kernel,
-        out_shape=first_shapes[3],
+        out_shape=first_shapes[5],
         in_specs=[VMEM_SPEC] * 2,
         out_specs=VMEM_SPEC,
         compiler_params=params,
         name="anchor",
-    )(state[3], totals[1])
-    state = (*state[:3], counts, state[4])
+    )(counts, totals[1])
     alpha, *totals = lax.optimization_barrier((alpha, *totals))
     swapped = moved(alpha, mate_of)
-    totals = view(1, alpha, weights_now, totals)
-    totals = view(2, swapped, weights_now, totals)
-    return view(3, beta, weights_now, totals, last=True)[0].transpose(1, 0, 2)
+    totals = view(1, alpha, counts_now, weights_now, totals)
+    totals = view(2, swapped, counts_now, weights_now, totals)
+    return view(3, beta, counts_now, weights_now, totals, last=True)[0].reshape(1, token_count, 3 * pixels)
 
 
 def solution(mesh):

time: 26.3 us -> 25.6 us (0.973)
  Pallas kernels: 16.1 us -> 15.5 us
    pallas_call x4, Pallas kernels: 13.2 us -> 12.7 us  [view(): pl.pallas_call(functools.partial(view_kernel, at, first, last), out_shape...]
  transfers between devices with their start and end apart: 4 -> 4, of which waited for: 1 -> 1; matrix products, arithmetic and copies ran while one was open for 0% -> 0% of each run, Pallas kernels for 46% -> 47%
where the time goes in v4:
time: 25.6 us; the launch traced here: 25.5 us
  Pallas kernels  15.5 us (61%)
  starting transfers between devices  6.82 us (27%)
  waiting for transfers between devices  3.09 us (12%)
    pallas_call x4, Pallas kernels, view(): pl.pallas_call(functools.partial(view_kernel, at, first, last), out_shape...  12.7 us
    ppermute x4, starting transfers between devices, moved(): lax.ppermute(value, 'scene', [(s, target_of(s) % scene_size) for s in ran...  6.82 us
    ppermute x4, waiting for transfers between devices, moved(): lax.ppermute(value, 'scene', [(s, target_of(s) % scene_size) for s in ran...  3.09 us
    pallas_call x1, Pallas kernels, per_device(): pl.pallas_call(functools.partial(first_kernel, scene_size, slots, offsets...  2.76 us
  transfers between devices with their start and end apart: 4, of which 1 were waited for; matrix products, arithmetic and copies ran while one was open for 0% of the time, Pallas kernels for 47%

profile of v4, /device:TPU:0, one launch (start us, length us, event | category | flops | bytes accessed | tf_op | source)
XLA Modules:
  0.0 25.5 jit_solution(16600860334688935337)
XLA Ops:
  0.0 0.5 %collective-permute-start = (bf16[196,768]{1,0:T(8,128)(2,1)}, bf16[196,768]{1,0:T(8,128)(2,1)S(1)}, u32[]{:S(2)}, u32[]{:S(2)}) collective-permute-start(bf16[196,768]{1,0:T(8,128)(2,1)} %bitcast.3), channel_id=1, source_target_pairs={{0,1},{1,0},{2,3},{3,2},{4,5},{5,4},{6,7},{7,6},{8,9},{9,8},{10,11... | collective-permute-start | bytes 903176 | tf_op jit(solution)/shard_map/ppermute | solution.py:250
  0.5 5.7 %collective-permute-start.2 = (bf16[196,768]{1,0:T(8,128)(2,1)}, bf16[196,768]{1,0:T(8,128)(2,1)S(1)}, u32[]{:S(2)}, u32[]{:S(2)}) collective-permute-start(bf16[196,768]{1,0:T(8,128)(2,1)} %bitcast.4), channel_id=1, source_target_pairs={{0,15},{1,2},{2,1},{3,4},{4,3},{5,6},{6,5},{7,8},{8,7},{9,10},{10,... | collective-permute-start | bytes 903176 | tf_op jit(solution)/shard_map/ppermute | solution.py:250
  6.1 2.8 %load_queries.1 = (bf16[196,768]{1,0:T(8,128)(2,1)S(1)}, bf16[196,768]{1,0:T(8,128)(2,1)S(1)}, bf16[768,1536]{1,0:T(8,128)(2,1)S(1)}, f32[2,768]{1,0:T(2,128)S(1...) custom-call(bf16[1,196,768]{2,1,0:T(8,128)(2,1)} %tokens_hbm.1, ...), custom_call_target="tpu_custom_call" | custom-call | flops 924844032 | bytes 1048576 | tf_op jit(solution)/shard_map/load_queries/pallas_call | solution.py:275
  8.9 0.0 collective-permute-done.partner_ref
  8.9 3.2 %shard_map.91 = (f32[196,768]{1,0:T(8,128)S(1)}, f32[196,256]{1,0:T(8,128)S(1)}, bf16[768,768]{1,0:T(8,128)(2,1)S(1)}, bf16[768,1024]{1,0:T(8,128)(2,1)S(1)}) custom-call(bf16[196,768]{1,0:T(8,128)(2,1)S(1)} %get-tuple-element.26.own_ref, f32[2,768]{1,0:T(2,128)S(1)} %get-tuple-element.27.gains_ref, f32[1,1024]{1,0:T(1,128)S(1)} %get-tuple-element.28.bias_ref, ...), custom_call_target="tpu_custom_call" | custom-call | flops 924844032 | bytes 1048576 | tf_op jit(solution)/shard_map/pallas_call | solution.py:309
  12.1 0.0 collective-permute-done.2.partner_ref
  12.1 0.1 collective-permute-start.3
  12.2 0.6 %collective-permute-start.1 = (bf16[196,768]{1,0:T(8,128)(2,1)S(1)}, bf16[196,768]{1,0:T(8,128)(2,1)S(1)}, u32[]{:S(2)}, u32[]{:S(2)}) collective-permute-start(bf16[196,768]{1,0:T(8,128)(2,1)S(1)} %get-tuple-element.38), channel_id=1, source_target_pairs={{0,2},{1,15},{2,4},{3,1},{4,6},{5,3},{6,8},{7,5},{8,10},{9,7},{10,... | collective-permute-start | bytes 903176 | tf_op jit(solution)/shard_map/ppermute | solution.py:250
  12.8 3.0 %shard_map.92 = (f32[196,768]{1,0:T(8,128)S(1)}, f32[196,256]{1,0:T(8,128)S(1)}) custom-call(bf16[196,768]{1,0:T(8,128)(2,1)S(1)} %get-tuple-element.26.own_ref, f32[2,768]{1,0:T(2,128)S(1)} %get-tuple-element.27.gains_ref, f32[1,1024]{1,0:T(1,128)S(1)} %get-tuple-element.28.bias_ref, f32[4,8,128]{2,1,0:T(8,128)S(1)} %anchor.1.counts_ref, ...), custom_call_target="tpu_custom_call" | custom-call | flops 924844032 | bytes 1048576 | tf_op jit(solution)/shard_map/pallas_call | solution.py:309
  15.8 0.0 collective-permute-done.3.partner_ref
  15.8 3.0 %shard_map.93 = (f32[196,768]{1,0:T(8,128)S(1)}, f32[196,256]{1,0:T(8,128)S(1)}) custom-call(bf16[196,768]{1,0:T(8,128)(2,1)S(1)} %get-tuple-element.26.own_ref, f32[2,768]{1,0:T(2,128)S(1)} %get-tuple-element.27.gains_ref, f32[1,1024]{1,0:T(1,128)S(1)} %get-tuple-element.28.bias_ref, f32[4,8,128]{2,1,0:T(8,128)S(1)} %anchor.1.counts_ref, ...), custom_call_target="tpu_custom_call" | custom-call | flops 924844032 | bytes 1048576 | tf_op jit(solution)/shard_map/pallas_call | solution.py:309
  18.8 3.1 %collective-permute-done.1.partner_ref = bf16[196,768]{1,0:T(8,128)(2,1)S(1)} collective-permute-done((bf16[196,768]{1,0:T(8,128)(2,1)S(1)}, bf16[196,768]{1,0:T(8,128)(2,1)S(1)}, u32[]{:S(2)}, u32[]{:S(2)}) %collective-permute-start.1) | collective-permute-done | bytes 301088 | tf_op jit(solution)/shard_map/ppermute | solution.py:250
  21.9 3.6 %shard_map.94 = f32[1176,128]{1,0:T(8,128)} custom-call(bf16[196,768]{1,0:T(8,128)(2,1)S(1)} %get-tuple-element.26.own_ref, f32[2,768]{1,0:T(2,128)S(1)} %get-tuple-element.27.gains_ref, f32[1,1024]{1,0:T(1,128)S(1)} %get-tuple-element.28.bias_ref, f32[4,8,128]{2,1,0:T(8,128)S(1)} %anchor.1.counts_ref, bf16[6,416,128]{2,1,0:T(8,128)(2,1)S(1)} %get-tuple-element.31.q_ref, ...), custom_call_target="tpu_custom_call" | custom-call | flops 924844032 | bytes 1048576 | tf_op jit(solution)/shard_map/pallas_call | solution.py:309
  (1 shorter events, 0.0 us)
Async XLA Ops:
  0.0 8.9 %collective-permute-start = (bf16[196,768]{1,0:T(8,128)(2,1)}, bf16[196,768]{1,0:T(8,128)(2,1)S(1)}, u32[]{:S(2)}, u32[]{:S(2)}) collective-permute-start(bf16[196,768]{1,0:T(8,128)(2,1)} %bitcast.3), channel_id=1, source_target_pairs={{0,1},{1,0},{2,3},{3,2},{4,5},{5,4},{6,7},{7,6},{8,9},{9,8},{10,11... | collective-permute-start | bytes 903176 | tf_op jit(solution)/shard_map/ppermute | solution.py:250
  0.5 11.6 %collective-permute-start.2 = (bf16[196,768]{1,0:T(8,128)(2,1)}, bf16[196,768]{1,0:T(8,128)(2,1)S(1)}, u32[]{:S(2)}, u32[]{:S(2)}) collective-permute-start(bf16[196,768]{1,0:T(8,128)(2,1)} %bitcast.4), channel_id=1, source_target_pairs={{0,15},{1,2},{2,1},{3,4},{4,3},{5,6},{6,5},{7,8},{8,7},{9,10},{10,... | collective-permute-start | bytes 903176 | tf_op jit(solution)/shard_map/ppermute | solution.py:250
  12.1 3.7 %collective-permute-start.3 = (bf16[196,768]{1,0:T(8,128)(2,1)S(1)}, bf16[196,768]{1,0:T(8,128)(2,1)S(1)}, u32[]{:S(2)}, u32[]{:S(2)}) collective-permute-start(bf16[196,768]{1,0:T(8,128)(2,1)S(1)} %collective-permute-done.2.partner_ref), channel_id=1, source_target_pairs={{0,1},{1,0},{2,3},{3,2},{4,5},{5,4},{6,7},{7,6},{8,9},{9,8},{10,11... | collective-permute-start | bytes 903176 | tf_op jit(solution)/shard_map/ppermute | solution.py:250
  12.2 9.7 %collective-permute-start.1 = (bf16[196,768]{1,0:T(8,128)(2,1)S(1)}, bf16[196,768]{1,0:T(8,128)(2,1)S(1)}, u32[]{:S(2)}, u32[]{:S(2)}) collective-permute-start(bf16[196,768]{1,0:T(8,128)(2,1)S(1)} %get-tuple-element.38), channel_id=1, source_target_pairs={{0,2},{1,15},{2,4},{3,1},{4,6},{5,3},{6,8},{7,5},{8,10},{9,7},{10,... | collective-permute-start | bytes 903176 | tf_op jit(solution)/shard_map/ppermute | solution.py:250

commit v5 on v4

--- a/solution.py
+++ b/solution.py
@@ -58,10 +58,9 @@
     return count
 
 
-def one_view(normed, count_row, own_ref, q_ref, kv_ref, out_ref, head_ref, gains_ref, bias_ref, keys_scr, vals_scr, att_scr, loads, emit):
-    tokens, width = own_ref.shape
+def attend(normed, q_ref, kv_ref, keys_scr, vals_scr, att_ref):
+    tokens, width = normed.shape
     head_size = width // HEADS
-    pixels = head_ref.shape[1] // 4
     rows = q_ref.shape[1] // 2
     padded = keys_scr.shape[0]
     pairs = width // LANES
@@ -92,10 +91,12 @@
         mixed = matmul(exponent, vals_scr[pair])
         top = jnp.where(low_head, mixed[:tokens, :LANES], mixed[rows : rows + tokens, :LANES])
         norm = jnp.where(low_head, mixed[:tokens, LANES:], mixed[rows : rows + tokens, LANES:])
-        att_scr[:, pair * LANES : (pair + 1) * LANES] = (top / norm).astype(jnp.bfloat16)
-    for load in loads:
-        load.wait()
-    mixed = own_ref[...].astype(jnp.float32) + matmul(att_scr[...], out_ref[...])
+        att_ref[:, pair * LANES : (pair + 1) * LANES] = (top / norm).astype(jnp.bfloat16)
+
+
+def finish(attended, count_row, own_ref, out_ref, head_ref, gains_ref, bias_ref, emit):
+    pixels = head_ref.shape[1] // 4
+    mixed = own_ref[...].astype(jnp.float32) + matmul(attended, out_ref[...])
     head_in = layer_norm(mixed, gains_ref[1:2, :]).astype(jnp.bfloat16)
     conf = matmul(head_in, head_ref[:, 3 * pixels :]) + bias_ref[:, 3 * pixels :]
     conf = conf.astype(jnp.bfloat16).astype(jnp.float32)
@@ -183,28 +184,30 @@
         counts_ref[at] = jnp.full(counts_ref.shape[1:], count, jnp.float32)
 
 
-def view_kernel(
-    at, first, last, own_ref, gains_ref, bias_ref, counts_ref, q_ref, kv_ref, out_ref, head_ref, partner_ref, *refs
-):
-    loads = ()
-    if first:
-        sums_ref, weights_ref, out_vmem, head_vmem, keys_scr, vals_scr, att_scr, load_sems = refs
-        loads = (
-            pltpu.make_async_copy(out_ref, out_vmem, load_sems.at[0]),
-            pltpu.make_async_copy(head_ref, head_vmem, load_sems.at[1]),
-        )
-        for load in loads:
-            load.start()
-        out_ref, head_ref = out_vmem, head_vmem
-    elif last:
+def mate_kernel(gains_ref, q_ref, kv_ref, partner_ref, att_ref, keys_scr, vals_scr):
+    normed = layer_norm(partner_ref[...].astype(jnp.float32), gains_ref[0:1, :]).astype(jnp.bfloat16)
+    attend(normed, q_ref, kv_ref, keys_scr, vals_scr, att_ref)
+
+
+def mate_maps_kernel(own_ref, gains_ref, bias_ref, counts_ref, att_ref, out_ref, head_ref, sums_ref, weights_ref):
+    def emit(part, cols, weight, weighted):
+        sums_ref[:, cols] = weighted
+        if part == 0:
+            weights_ref[...] = weight
+
+    finish(att_ref[...], counts_ref[0, 0:1, 0:1], own_ref, out_ref, head_ref, gains_ref, bias_ref, emit)
+
+
+def view_kernel(at, last, own_ref, gains_ref, bias_ref, counts_ref, q_ref, kv_ref, out_ref, head_ref, partner_ref, *refs):
+    if last:
         sums_in, weights_in, joined_hbm, keys_scr, vals_scr, att_scr, joined_scr, sems = refs
     else:
         sums_in, weights_in, sums_ref, weights_ref, keys_scr, vals_scr, att_scr = refs
     copies = []
 
     def emit(part, cols, weight, weighted):
-        total = weighted if first else sums_in[:, cols] + weighted
-        weight = weight if first else weights_in[...] + weight
+        total = sums_in[:, cols] + weighted
+        weight = weights_in[...] + weight
         if last:
             ratio = total / weight
             lines = 3 * total.shape[1] // LANES
@@ -223,16 +226,10 @@
     normed = partner_ref[...]
     if not last:
         normed = layer_norm(normed.astype(jnp.float32), gains_ref[0:1, :]).astype(jnp.bfloat16)
-    one_view(
-        normed, counts_ref[at, 0:1, 0:1], own_ref, q_ref, kv_ref, out_ref, head_ref, gains_ref, bias_ref,
-        keys_scr, vals_scr, att_scr, loads, emit,
-    )
+    attend(normed, q_ref, kv_ref, keys_scr, vals_scr, att_scr)
+    finish(att_scr[...], counts_ref[at, 0:1, 0:1], own_ref, out_ref, head_ref, gains_ref, bias_ref, emit)
     for copy in copies:
         copy.wait()
-
-
-def anchor_kernel(counts_in, weights_ref, counts_ref):
-    counts_ref[...] = counts_in[...]
 
 
 def per_device(
@@ -293,46 +290,58 @@
         in_hbm(pair_count),
     )
 
-    def view(at, partner, counts_now, weights_now, totals, last=False):
-        first = not totals
-        operands = [own_vmem, gains, bias, counts_now, queries, kv_vmem, *weights_now, partner, *totals]
-        in_specs = [VMEM_SPEC] * len(operands)
-        scratch = view_scratch(token_count, width)
-        out_shape = [sums, weights]
-        if first:
-            out_shape += [jax.ShapeDtypeStruct(value.shape, value.dtype) for value in weights_now]
-            in_specs[6:8] = [HBM_SPEC] * 2
-            scratch += [pltpu.SemaphoreType.DMA((2,))]
-        if last:
-            out_shape = [jax.ShapeDtypeStruct((token_count * 3 * pixels // LANES, LANES), f32)]
-            scratch += [pltpu.VMEM(out_shape[0].shape, f32), pltpu.SemaphoreType.DMA((1,))]
+    def kernel(body, operands, in_specs, out_shape, out_spec, scratch):
         return pl.pallas_call(
-            functools.partial(view_kernel, at, first, last),
+            body,
             out_shape=out_shape,
             in_specs=in_specs,
-            out_specs=[HBM_SPEC if last else VMEM_SPEC] * len(out_shape),
+            out_specs=[out_spec] * len(out_shape),
             scratch_shapes=scratch,
             compiler_params=params,
             cost_estimate=cost,
         )(*operands)
 
-    *totals, out_vmem, head_vmem = view(0, mate, counts, (in_hbm(out_weight), in_hbm(head_weight)), ())
-    weights_now = (out_vmem, head_vmem)
-    normed, *totals = lax.optimization_barrier((normed, *totals))
+    scratch = view_scratch(token_count, width)
+    (attended,) = kernel(
+        mate_kernel,
+        (gains, queries, kv_vmem, mate),
+        [VMEM_SPEC] * 4,
+        [jax.ShapeDtypeStruct((token_count, width), bf16)],
+        VMEM_SPEC,
+        scratch[:2],
+    )
+    normed, attended = lax.optimization_barrier((normed, attended))
     beta = moved(normed, lambda s: s - 2 if s % 2 else s + 2)
-    counts_now = pl.pallas_call(
-        anchor_kernel,
-        out_shape=first_shapes[5],
-        in_specs=[VMEM_SPEC] * 2,
-        out_specs=VMEM_SPEC,
-        compiler_params=params,
-        name="anchor",
-    )(counts, totals[1])
+    totals = kernel(
+        mate_maps_kernel,
+        (own_vmem, gains, bias, counts, attended, out_weight, head_weight),
+        [VMEM_SPEC] * 7,
+        (sums, weights),
+        VMEM_SPEC,
+        [],
+    )
     alpha, *totals = lax.optimization_barrier((alpha, *totals))
     swapped = moved(alpha, mate_of)
-    totals = view(1, alpha, counts_now, weights_now, totals)
-    totals = view(2, swapped, counts_now, weights_now, totals)
-    return view(3, beta, counts_now, weights_now, totals, last=True)[0].reshape(1, token_count, 3 * pixels)
+    common = (own_vmem, gains, bias, counts, queries, kv_vmem, out_weight, head_weight)
+    for at, partner in ((1, alpha), (2, swapped)):
+        totals = kernel(
+            functools.partial(view_kernel, at, False),
+            (*common, partner, *totals),
+            [VMEM_SPEC] * 11,
+            (sums, weights),
+            VMEM_SPEC,
+            scratch,
+        )
+    joined_shape = jax.ShapeDtypeStruct((token_count * 3 * pixels // LANES, LANES), f32)
+    (joined,) = kernel(
+        functools.partial(view_kernel, 3, True),
+        (*common, beta, *totals),
+        [VMEM_SPEC] * 11,
+        (joined_shape,),
+        HBM_SPEC,
+        scratch + [pltpu.VMEM(joined_shape.shape, f32), pltpu.SemaphoreType.DMA((1,))],
+    )
+    return joined.reshape(1, token_count, 3 * pixels)
 
 
 def solution(mesh):

time: 25.6 us -> 25.7 us (level)
  transfers between devices with their start and end apart: 4 -> 4, of which waited for: 1 -> 1; matrix products, arithmetic and copies ran while one was open for 0% -> 0% of each run, Pallas kernels for 47% -> 46%
where the time goes in v5:
time: 25.7 us; the launch traced here: 25.5 us
  Pallas kernels  15.5 us (60%)
  starting transfers between devices  6.81 us (26%)
  waiting for transfers between devices  3.11 us (12%)
    pallas_call x5, Pallas kernels, kernel(): pl.pallas_call(body, out_shape=out_shape, in_specs=in_specs, out_specs=[o...  12.7 us
    ppermute x4, starting transfers between devices, moved(): lax.ppermute(value, 'scene', [(s, target_of(s) % scene_size) for s in ran...  6.81 us
    ppermute x4, waiting for transfers between devices, moved(): lax.ppermute(value, 'scene', [(s, target_of(s) % scene_size) for s in ran...  3.11 us
    pallas_call x1, Pallas kernels, per_device(): pl.pallas_call(functools.partial(first_kernel, scene_size, slots, offsets...  2.76 us
  transfers between devices with their start and end apart: 4, of which 1 were waited for; matrix products, arithmetic and copies ran while one was open for 0% of the time, Pallas kernels for 46%

profile of v5, /device:TPU:0, one launch (start us, length us, event | category | flops | bytes accessed | tf_op | source)
XLA Modules:
  0.0 25.5 jit_solution(2020589275204224493)
XLA Ops:
  0.0 0.5 %collective-permute-start = (bf16[196,768]{1,0:T(8,128)(2,1)}, bf16[196,768]{1,0:T(8,128)(2,1)S(1)}, u32[]{:S(2)}, u32[]{:S(2)}) collective-permute-start(bf16[196,768]{1,0:T(8,128)(2,1)} %bitcast.3), channel_id=1, source_target_pairs={{0,1},{1,0},{2,3},{3,2},{4,5},{5,4},{6,7},{7,6},{8,9},{9,8},{10,11... | collective-permute-start | bytes 903176 | tf_op jit(solution)/shard_map/ppermute | solution.py:247
  0.5 5.7 %collective-permute-start.2 = (bf16[196,768]{1,0:T(8,128)(2,1)}, bf16[196,768]{1,0:T(8,128)(2,1)S(1)}, u32[]{:S(2)}, u32[]{:S(2)}) collective-permute-start(bf16[196,768]{1,0:T(8,128)(2,1)} %bitcast.4), channel_id=1, source_target_pairs={{0,15},{1,2},{2,1},{3,4},{4,3},{5,6},{6,5},{7,8},{8,7},{9,10},{10,... | collective-permute-start | bytes 903176 | tf_op jit(solution)/shard_map/ppermute | solution.py:247
  6.1 2.8 %load_queries.1 = (bf16[196,768]{1,0:T(8,128)(2,1)S(1)}, bf16[196,768]{1,0:T(8,128)(2,1)S(1)}, bf16[768,1536]{1,0:T(8,128)(2,1)S(1)}, f32[2,768]{1,0:T(2,128)S(1...) custom-call(bf16[1,196,768]{2,1,0:T(8,128)(2,1)} %tokens_hbm.1, ...), custom_call_target="tpu_custom_call" | custom-call | flops 924844032 | bytes 1048576 | tf_op jit(solution)/shard_map/load_queries/pallas_call | solution.py:272
  8.9 0.0 copy-start
  8.9 0.0 copy-start.1
  8.9 0.0 collective-permute-done.partner_ref
  9.0 1.9 %shard_map.91.att_ref = bf16[196,768]{1,0:T(8,128)(2,1)S(1)} custom-call(f32[2,768]{1,0:T(2,128)S(1)} %get-tuple-element.24.gains_ref, bf16[6,416,128]{2,1,0:T(8,128)(2,1)S(1)} %get-tuple-element.27.q_ref, bf16[768,1536]{1,0:T(8,128)(2,1)S(1)} %get-tuple-element.28.kv_ref, bf16[196,768]{1,0:T(8,128)(2,1)S(1)} %collective-permute-done.partner_ref), custom_call_target="tpu_custom_call" | custom-call | flops 924844032 | bytes 1048576 | tf_op jit(solution)/shard_map/pallas_call | solution.py:294
  10.9 0.0 copy-done
  10.9 0.0 copy-done.1
  10.9 1.2 %shard_map.92 = (f32[196,768]{1,0:T(8,128)S(1)}, f32[196,256]{1,0:T(8,128)S(1)}) custom-call(bf16[196,768]{1,0:T(8,128)(2,1)S(1)} %get-tuple-element.23.own_ref, f32[2,768]{1,0:T(2,128)S(1)} %get-tuple-element.24.gains_ref, f32[1,1024]{1,0:T(1,128)S(1)} %get-tuple-element.25.bias_ref, f32[4,8,128]{2,1,0:T(8,128)S(1)} %get-tuple-element.26.counts_ref, ...), custom_call_target="tpu_custom_call" | custom-call | flops 924844032 | bytes 1048576 | tf_op jit(solution)/shard_map/pallas_call | solution.py:294
  12.1 0.0 collective-permute-done.2.partner_ref
  12.1 0.1 collective-permute-start.3
  12.2 0.6 %collective-permute-start.1 = (bf16[196,768]{1,0:T(8,128)(2,1)S(1)}, bf16[196,768]{1,0:T(8,128)(2,1)S(1)}, u32[]{:S(2)}, u32[]{:S(2)}) collective-permute-start(bf16[196,768]{1,0:T(8,128)(2,1)S(1)} %get-tuple-element.30), channel_id=1, source_target_pairs={{0,2},{1,15},{2,4},{3,1},{4,6},{5,3},{6,8},{7,5},{8,10},{9,7},{10,... | collective-permute-start | bytes 903176 | tf_op jit(solution)/shard_map/ppermute | solution.py:247
  12.8 3.0 %shard_map.93 = (f32[196,768]{1,0:T(8,128)S(1)}, f32[196,256]{1,0:T(8,128)S(1)}) custom-call(bf16[196,768]{1,0:T(8,128)(2,1)S(1)} %get-tuple-element.23.own_ref, f32[2,768]{1,0:T(2,128)S(1)} %get-tuple-element.24.gains_ref, f32[1,1024]{1,0:T(1,128)S(1)} %get-tuple-element.25.bias_ref, f32[4,8,128]{2,1,0:T(8,128)S(1)} %get-tuple-element.26.counts_ref, ...), custom_call_target="tpu_custom_call" | custom-call | flops 924844032 | bytes 1048576 | tf_op jit(solution)/shard_map/pallas_call | solution.py:294
  15.8 0.0 collective-permute-done.3.partner_ref
  15.8 3.0 %shard_map.94 = (f32[196,768]{1,0:T(8,128)S(1)}, f32[196,256]{1,0:T(8,128)S(1)}) custom-call(bf16[196,768]{1,0:T(8,128)(2,1)S(1)} %get-tuple-element.23.own_ref, f32[2,768]{1,0:T(2,128)S(1)} %get-tuple-element.24.gains_ref, f32[1,1024]{1,0:T(1,128)S(1)} %get-tuple-element.25.bias_ref, f32[4,8,128]{2,1,0:T(8,128)S(1)} %get-tuple-element.26.counts_ref, ...), custom_call_target="tpu_custom_call" | custom-call | flops 924844032 | bytes 1048576 | tf_op jit(solution)/shard_map/pallas_call | solution.py:294
  18.8 3.1 %collective-permute-done.1.partner_ref = bf16[196,768]{1,0:T(8,128)(2,1)S(1)} collective-permute-done((bf16[196,768]{1,0:T(8,128)(2,1)S(1)}, bf16[196,768]{1,0:T(8,128)(2,1)S(1)}, u32[]{:S(2)}, u32[]{:S(2)}) %collective-permute-start.1) | collective-permute-done | bytes 301088 | tf_op jit(solution)/shard_map/ppermute | solution.py:247
  21.9 3.6 %shard_map.95 = f32[1176,128]{1,0:T(8,128)} custom-call(bf16[196,768]{1,0:T(8,128)(2,1)S(1)} %get-tuple-element.23.own_ref, f32[2,768]{1,0:T(2,128)S(1)} %get-tuple-element.24.gains_ref, f32[1,1024]{1,0:T(1,128)S(1)} %get-tuple-element.25.bias_ref, f32[4,8,128]{2,1,0:T(8,128)S(1)} %get-tuple-element.26.counts_ref, ...), custom_call_target="tpu_custom_call" | custom-call | flops 924844032 | bytes 1048576 | tf_op jit(solution)/shard_map/pallas_call | solution.py:294
Async XLA Ops:
  0.0 8.9 %collective-permute-start = (bf16[196,768]{1,0:T(8,128)(2,1)}, bf16[196,768]{1,0:T(8,128)(2,1)S(1)}, u32[]{:S(2)}, u32[]{:S(2)}) collective-permute-start(bf16[196,768]{1,0:T(8,128)(2,1)} %bitcast.3), channel_id=1, source_target_pairs={{0,1},{1,0},{2,3},{3,2},{4,5},{5,4},{6,7},{7,6},{8,9},{9,8},{10,11... | collective-permute-start | bytes 903176 | tf_op jit(solution)/shard_map/ppermute | solution.py:247
  0.5 11.6 %collective-permute-start.2 = (bf16[196,768]{1,0:T(8,128)(2,1)}, bf16[196,768]{1,0:T(8,128)(2,1)S(1)}, u32[]{:S(2)}, u32[]{:S(2)}) collective-permute-start(bf16[196,768]{1,0:T(8,128)(2,1)} %bitcast.4), channel_id=1, source_target_pairs={{0,15},{1,2},{2,1},{3,4},{4,3},{5,6},{6,5},{7,8},{8,7},{9,10},{10,... | collective-permute-start | bytes 903176 | tf_op jit(solution)/shard_map/ppermute | solution.py:247
  8.9 2.0 %copy-start = (bf16[768,1024]{1,0:T(8,128)(2,1)S(1)}, bf16[768,1024]{1,0:T(8,128)(2,1)}, u32[]{:S(2)}) copy-start(bf16[768,1024]{1,0:T(8,128)(2,1)} %head_ref.7) | copy-start | bytes 4718596
  8.9 2.0 %copy-start.1 = (bf16[768,768]{1,0:T(8,128)(2,1)S(1)}, bf16[768,768]{1,0:T(8,128)(2,1)}, u32[]{:S(2)}) copy-start(bf16[768,768]{1,0:T(8,128)(2,1)} %out_ref.7) | copy-start | bytes 3538948
  12.1 3.7 %collective-permute-start.3 = (bf16[196,768]{1,0:T(8,128)(2,1)S(1)}, bf16[196,768]{1,0:T(8,128)(2,1)S(1)}, u32[]{:S(2)}, u32[]{:S(2)}) collective-permute-start(bf16[196,768]{1,0:T(8,128)(2,1)S(1)} %collective-permute-done.2.partner_ref), channel_id=1, source_target_pairs={{0,1},{1,0},{2,3},{3,2},{4,5},{5,4},{6,7},{7,6},{8,9},{9,8},{10,11... | collective-permute-start | bytes 903176 | tf_op jit(solution)/shard_map/ppermute | solution.py:247
  12.2 9.7 %collective-permute-start.1 = (bf16[196,768]{1,0:T(8,128)(2,1)S(1)}, bf16[196,768]{1,0:T(8,128)(2,1)S(1)}, u32[]{:S(2)}, u32[]{:S(2)}) collective-permute-start(bf16[196,768]{1,0:T(8,128)(2,1)S(1)} %get-tuple-element.30), channel_id=1, source_target_pairs={{0,2},{1,15},{2,4},{3,1},{4,6},{5,3},{6,8},{7,5},{8,10},{9,7},{10,... | collective-permute-start | bytes 903176 | tf_op jit(solution)/shard_map/ppermute | solution.py:247
